TPU v7x, 32 devices: a whole 2x2x4 slice. The times are simulated.
32 devices in a mesh: dp: 4 (over y, core), row: 4 (over z), col: 2 (over x).
Axes of the slice: x: 2, y: 2, z: 4, core: 2. Of those that a mesh axis runs over, the one named last changes fastest.
Arguments:
- tokens: bfloat16 [768, 4096], P('row', ('dp', 'col')), may hold values from -6 to 6
- segment_ids: int32 [16, 256], P(('dp', 'row')), may hold values from 0 to 7, never falling along the last dimension, each value on 1 to 96 neighbouring positions
- query_weight: bfloat16 [768, 768], P('row', 'col'), may hold values from -0.21875 to 0.21875
- key_weight: bfloat16 [768, 768], P('row', 'col'), may hold values from -0.21875 to 0.21875
- value_weight: bfloat16 [768, 768], P('row', 'col'), may hold values from -0.21875 to 0.21875
- query_bias: float32 [768], P('col'), may hold values from -3 to 3
- value_bias: float32 [768], P('col'), may hold values from -3 to 3
- out_weight: bfloat16 [768, 768], P('col', 'row'), may hold values from -0.875 to 0.875
- out_bias: float32 [768], P('row'), may hold values from -3 to 3
- attn_gain: float32 [768], P('row'), may hold values from 0.5 to 1.5
- attn_shift: float32 [768], P('row'), may hold values from -3 to 3
- up_weight: bfloat16 [768, 3072], P('row', 'col'), may hold values from -0.21875 to 0.21875
- up_bias: float32 [3072], P('col'), may hold values from -3 to 3
- down_weight: bfloat16 [3072, 768], P('col', 'row'), may hold values from -0.109375 to 0.109375
- down_bias: float32 [768], P('row'), may hold values from -3 to 3
- ffn_gain: float32 [768], P('row'), may hold values from 0.5 to 1.5
- ffn_shift: float32 [768], P('row'), may hold values from -3 to 3
- cotangent: bfloat16 [768, 4096], P('row', ('dp', 'col')), may hold values from -6 to 6
Outputs:
- output: bfloat16 [768, 4096], P('row', ('dp', 'col'))
- tokens_grad: float32 [768, 4096], P('row', ('dp', 'col'))
- query_weight_grad: float32 [768, 768], P('row', 'col')
- key_weight_grad: float32 [768, 768], P('row', 'col')
- value_weight_grad: float32 [768, 768], P('row', 'col')
- query_bias_grad: float32 [768], P('col')
- value_bias_grad: float32 [768], P('col')
- out_weight_grad: float32 [768, 768], P('col', 'row')
- out_bias_grad: float32 [768], P('row')
- attn_gain_grad: float32 [768], P('row')
- attn_shift_grad: float32 [768], P('row')
- up_weight_grad: float32 [768, 3072], P('row', 'col')
- up_bias_grad: float32 [3072], P('col')
- down_weight_grad: float32 [3072, 768], P('col', 'row')
- down_bias_grad: float32 [768], P('row')
- ffn_gain_grad: float32 [768], P('row')
- ffn_shift_grad: float32 [768], P('row')
Inputs may be any that keep to these rules, and one draw needn't show every extreme that they name: `segment_ids`: in each row segment numbers never fall and start at 0; each document has 1 to 96 tokens, and one has exactly that many.
All inputs are finite; a program needn't handle non-finite values.
Results may differ from a plain program's by a relative error of at most 0.012.
Values may be sent and summed in bfloat16 or wider, within the bound.
A program may use at most 128 MiB of HBM per device.

v0:
```python
import math

import jax
import jax.numpy as jnp
from jax import lax
from jax.sharding import PartitionSpec as P

HEADS = 12
HEAD = 64


EPS = 1e-05


def gather_over_col(values):
    return lax.all_gather(values, "col", axis=0, tiled=True)


def gather_over_row(values):
    return lax.all_gather(values, "row", axis=0, tiled=True)


def contract(left, weight, flipped):
    if flipped:
        return lax.dot_general(
            left, weight, (((1,), (1,)), ((), ())), preferred_element_type=jnp.float32
        )
    return jnp.dot(left, weight, preferred_element_type=jnp.float32)


def product_rows(gathered, weight, flipped):
    return contract(gathered, weight, flipped)


def heads_in(values):
    return lax.all_to_all(values, "col", split_axis=0, concat_axis=1, tiled=True)


def heads_out(values):
    return lax.all_to_all(values, "col", split_axis=1, concat_axis=0, tiled=True)


def sum_over_row(gathered, block, flipped):
    return lax.psum_scatter(
        product_rows(gathered, block, flipped), "row", scatter_dimension=0, tiled=True
    )


def sum_over_col(gathered, block, flipped):
    return lax.psum_scatter(
        product_rows(gathered, block, flipped), "col", scatter_dimension=0, tiled=True
    )


def row_totals(values):
    return lax.psum(values, "row")


def layer_norm(resid, gain, shift):
    feature_count = resid.shape[1] * lax.axis_size("row")
    centre = row_totals((jnp.sum(resid, 1, keepdims=True),))[0] / feature_count
    deviate = resid - centre
    spread = row_totals((jnp.sum(deviate * deviate, 1, keepdims=True),))[0] / feature_count
    scaling = lax.rsqrt(spread + EPS)
    normed = deviate * scaling
    return (normed * gain + shift, normed, scaling)


def norm_backward(upstream, normed, scaling, gain):
    feature_count = upstream.shape[1] * lax.axis_size("row")
    scaled_grad = upstream * gain
    first_sum, second_sum = row_totals(
        (jnp.sum(scaled_grad, 1, keepdims=True), jnp.sum(scaled_grad * normed, 1, keepdims=True))
    )
    return scaling * (
        scaled_grad - first_sum / feature_count - normed * (second_sum / feature_count)
    )


def gelu_tanh(values):
    return jax.nn.gelu(values, approximate=True)


def column_sums(values):
    return jnp.sum(values, 0, dtype=jnp.float32)


def head_scores(query_split, key_split, same_doc):
    scores = jnp.einsum("qhd,khd->hqk", query_split, key_split, preferred_element_type=jnp.float32)
    scores = scores * (1.0 / math.sqrt(HEAD))
    return jnp.where(same_doc[None], scores, -1000000000.0)


def body(
    tokens,
    segment_ids,
    query_weight,
    key_weight,
    value_weight,
    query_bias,
    value_bias,
    out_weight,
    out_bias,
    attn_gain,
    attn_shift,
    up_weight,
    up_bias,
    down_weight,
    down_bias,
    ffn_gain,
    ffn_shift,
    cotangent,
):
    token_major = tokens.T
    head_cols = query_weight.shape[1]
    score_scale = 1.0 / math.sqrt(HEAD)
    joined_weight = jnp.concatenate([query_weight, key_weight, value_weight], 1)
    token_rows = gather_over_col(token_major)
    joined = sum_over_row(token_rows, joined_weight, False)
    query_block = (joined[:, :head_cols] + query_bias).astype(jnp.bfloat16)
    key_block = joined[:, head_cols : 2 * head_cols].astype(jnp.bfloat16)
    value_block = (joined[:, 2 * head_cols :] + value_bias).astype(jnp.bfloat16)
    query_heads = heads_in(query_block)
    key_heads, value_heads = (
        lax.all_gather(key_block, "col", axis=1, tiled=True),
        lax.all_gather(value_block, "col", axis=1, tiled=True),
    )
    query_count = query_heads.shape[0]
    key_count = key_heads.shape[0]
    sequence_ids = segment_ids[0]
    query_ids = lax.dynamic_slice_in_dim(
        sequence_ids, lax.axis_index("col") * query_count, query_count, 0
    )
    same_doc = query_ids[:, None] == sequence_ids[None, :]
    query_split = query_heads.reshape(query_count, HEADS, HEAD)
    key_split = key_heads.reshape(key_count, HEADS, HEAD)
    value_split = value_heads.reshape(key_count, HEADS, HEAD)
    scores = head_scores(query_split, key_split, same_doc)
    highest = jnp.max(scores, -1, keepdims=True)
    exponent = jnp.exp(scores - highest)
    totals = jnp.sum(exponent, -1, keepdims=True)
    log_totals = highest + jnp.log(totals)
    attn_probs = (exponent / totals).astype(jnp.bfloat16)
    attended = jnp.einsum(
        "hqk,khd->qhd", attn_probs, value_split, preferred_element_type=jnp.float32
    )
    attended = attended.reshape(query_count, -1).astype(jnp.bfloat16)
    attended_block = heads_out(attended)
    attended_rows = gather_over_row(attended_block)
    projected = sum_over_col(attended_rows, out_weight, False) + out_bias
    hidden, hidden_normed, hidden_scaling = layer_norm(
        token_major.astype(jnp.float32) + projected, attn_gain, attn_shift
    )
    hidden_low = hidden.astype(jnp.bfloat16)
    hidden_rows = gather_over_col(hidden_low)
    pre_act = sum_over_row(hidden_rows, up_weight, False) + up_bias
    activated, gelu_pull = jax.vjp(gelu_tanh, pre_act)
    act_block = activated.astype(jnp.bfloat16)
    act_rows = gather_over_row(act_block)
    down_out = sum_over_col(act_rows, down_weight, False) + down_bias
    output, out_normed, out_scaling = layer_norm(hidden + down_out, ffn_gain, ffn_shift)
    upstream = cotangent.T.astype(jnp.float32)
    ffn_gain_grad = jnp.sum(upstream * out_normed, 0)
    ffn_shift_grad = jnp.sum(upstream, 0)
    resid_grad = norm_backward(upstream, out_normed, out_scaling, ffn_gain)
    down_grad_rows = gather_over_col(resid_grad.astype(jnp.bfloat16))
    down_weight_grad = jnp.einsum(
        "tf,td->fd", act_rows, down_grad_rows, preferred_element_type=jnp.float32
    )
    down_bias_grad = column_sums(down_grad_rows)
    act_grad = sum_over_row(down_grad_rows, down_weight, True)
    pre_grad = gelu_pull(act_grad)[0].astype(jnp.bfloat16)
    pre_grad_rows = gather_over_row(pre_grad)
    up_weight_grad = jnp.einsum(
        "td,tf->df", hidden_rows, pre_grad_rows, preferred_element_type=jnp.float32
    )
    up_bias_grad = column_sums(pre_grad_rows)
    hidden_grad = sum_over_col(pre_grad_rows, up_weight, True) + resid_grad
    attn_gain_grad = jnp.sum(hidden_grad * hidden_normed, 0)
    attn_shift_grad = jnp.sum(hidden_grad, 0)
    first_grad = norm_backward(hidden_grad, hidden_normed, hidden_scaling, attn_gain)
    proj_grad_rows = gather_over_col(first_grad.astype(jnp.bfloat16))
    out_weight_grad = jnp.einsum(
        "tc,td->cd", attended_rows, proj_grad_rows, preferred_element_type=jnp.float32
    )
    out_bias_grad = column_sums(proj_grad_rows)
    attended_grad = heads_in(sum_over_row(proj_grad_rows, out_weight, True).astype(jnp.bfloat16))
    scores = head_scores(query_split, key_split, same_doc)
    attn_exact = jnp.exp(scores - log_totals)
    grad_split = attended_grad.reshape(query_count, HEADS, HEAD)
    prob_grad = jnp.einsum(
        "qhd,khd->hqk", grad_split, value_split, preferred_element_type=jnp.float32
    )
    score_grad = attn_exact * (prob_grad - jnp.sum(prob_grad * attn_exact, -1, keepdims=True))
    score_grad = score_grad.astype(jnp.bfloat16)
    query_grad = (
        jnp.einsum("hqk,khd->qhd", score_grad, key_split, preferred_element_type=jnp.float32)
        * score_scale
    )
    query_grad = query_grad.reshape(query_count, -1).astype(jnp.bfloat16)
    key_grad = (
        jnp.einsum("hqk,qhd->khd", score_grad, query_split, preferred_element_type=jnp.float32)
        * score_scale
    )
    key_grad = key_grad.reshape(key_count, -1)
    value_grad = jnp.einsum(
        "hqk,qhd->khd",
        attn_exact.astype(jnp.bfloat16),
        grad_split,
        preferred_element_type=jnp.float32,
    ).reshape(key_count, -1)
    key_sum, value_sum = (
        lax.psum_scatter(
            key_grad.astype(jnp.bfloat16), "col", scatter_dimension=1, tiled=True
        ).astype(jnp.float32),
        lax.psum_scatter(
            value_grad.astype(jnp.bfloat16), "col", scatter_dimension=1, tiled=True
        ).astype(jnp.float32),
    )
    joined_grad = jnp.concatenate(
        [heads_out(query_grad), key_sum.astype(jnp.bfloat16), value_sum.astype(jnp.bfloat16)], 1
    )
    joined_rows = gather_over_row(joined_grad)
    joined_weight_grad = jnp.einsum(
        "td,tf->df", token_rows, joined_rows, preferred_element_type=jnp.float32
    )
    query_bias_grad = column_sums(joined_rows[:, :head_cols])
    value_bias_grad = column_sums(joined_rows[:, 2 * head_cols :])
    tokens_grad = sum_over_col(joined_rows, joined_weight, True) + first_grad
    summed = lax.psum(
        (
            joined_weight_grad,
            query_bias_grad,
            value_bias_grad,
            out_weight_grad,
            out_bias_grad,
            up_weight_grad,
            up_bias_grad,
            down_weight_grad,
            down_bias_grad,
        ),
        "dp",
    )
    norm_sums = lax.psum(
        (attn_gain_grad, attn_shift_grad, ffn_gain_grad, ffn_shift_grad), ("dp", "col")
    )
    return (
        output.T.astype(jnp.bfloat16),
        tokens_grad.T,
        summed[0][:, :head_cols],
        summed[0][:, head_cols : 2 * head_cols],
        summed[0][:, 2 * head_cols :],
        summed[1],
        summed[2],
        summed[3],
        summed[4],
        norm_sums[0],
        norm_sums[1],
        summed[5],
        summed[6],
        summed[7],
        summed[8],
        norm_sums[2],
        norm_sums[3],
    )


def solution(mesh):
    placed = (
        P("row", ("dp", "col")),
        P(("dp", "row"), None),
        P("row", "col"),
        P("row", "col"),
        P("row", "col"),
        P("col"),
        P("col"),
        P("col", "row"),
        P("row"),
        P("row"),
        P("row"),
        P("row", "col"),
        P("col"),
        P("col", "row"),
        P("row"),
        P("row"),
        P("row"),
        P("row", ("dp", "col")),
    )
    return jax.shard_map(
        body,
        mesh=mesh,
        in_specs=placed,
        out_specs=(
            P("row", ("dp", "col")),
            P("row", ("dp", "col")),
            P("row", "col"),
            P("row", "col"),
            P("row", "col"),
            P("col"),
            P("col"),
            P("col", "row"),
            P("row"),
            P("row"),
            P("row"),
            P("row", "col"),
            P("col"),
            P("col", "row"),
            P("row"),
            P("row"),
            P("row"),
        ),
        check_vma=False,
    )
```

profile of v0, /device:TPU:17, one launch (start us, length us, event | category | flops | bytes accessed | tf_op | source)
XLA Modules:
  0.0 904.7 jit_solution(11849187131845979183)
XLA Ops:
  7.2 6.8 all_gather.30
  17.0 2.9 convolution_bitcast_fusion
  20.7 87.1 %reduce-scatter.15.cloned.1.call-done = f32[256,1152]{0,1:T(8,128)} async-done(((f32[1024,1152]{0,1:T(8,128)}), f32[256,1152]{0,1:T(8,128)}) %reduce-scatter.15.cloned.1.call-update) | async-done | bytes 1179664 | tf_op jit(solution)/shard_map/reduce_scatter | solution.py:44
  109.8 3.4 all-to-all-start
  114.3 7.6 all_gather.32
  121.9 6.0 all_gather.31
  129.9 6.1 all_to_all.64
  136.0 14.8 %all_gather.33 = bf16[1024,384]{1,0:T(8,128)(2,1)S(1)} all-gather(bf16[256,384]{1,0:T(8,128)(2,1)S(1)} %bitcast.140), channel_id=1, replica_groups=mesh['dp'=4,'row'=4,'col'=2] {'row'}, dimensions={0}, use_global_device_ids=true | all-gather | bytes 983040 | tf_op jit(solution)/shard_map/all_gather | solution.py:20
  153.1 21.8 %reduce-scatter.17.cloned.1.call-done = f32[512,192]{0,1:T(8,128)} async-done(((f32[1024,192]{0,1:T(8,128)}), f32[512,192]{0,1:T(8,128)}) %reduce-scatter.17.cloned.1.call-update) | async-done | bytes 393232 | tf_op jit(solution)/shard_map/reduce_scatter | solution.py:50
  176.1 6.9 psum.147
  183.0 7.3 psum.148
  190.5 5.2 all_gather.34
  196.4 3.7 fusion.36
  200.2 117.2 %reduce-scatter.19.cloned.1.call-done = f32[256,1536]{1,0:T(8,128)} async-done(((f32[1024,1536]{1,0:T(8,128)}), f32[256,1536]{1,0:T(8,128)}) %reduce-scatter.19.cloned.1.call-update) | async-done | bytes 1572880 | tf_op jit(solution)/shard_map/reduce_scatter | solution.py:44
  317.4 2.8 multiply_convert_fusion.1
  320.4 62.1 %all-gather.4.cloned.1.call-done = bf16[1024,1536]{1,0:T(8,128)(2,1)} async-done(((bf16[256,1536]{1,0:T(8,128)(2,1)}), bf16[1024,1536]{1,0:T(8,128)(2,1)}) %all-gather.4.cloned.1.call-update) | async-done | bytes 3145744 | tf_op jit(solution)/shard_map/all_gather | solution.py:20
  382.4 3.9 fusion.37
  386.4 17.6 %reduce-scatter.21.cloned.1.call-done = f32[512,192]{0,1:T(8,128)} async-done(((f32[1024,192]{0,1:T(8,128)}), f32[512,192]{0,1:T(8,128)}) %reduce-scatter.21.cloned.1.call-update) | async-done | bytes 393232 | tf_op jit(solution)/shard_map/reduce_scatter | solution.py:50
  405.2 6.9 psum.149
  412.2 7.3 psum.150
  420.3 7.6 all-reduce.2
  428.7 5.4 all_gather.36
  434.1 3.7 fusion.38
  437.9 118.2 %reduce-scatter.23.cloned.1.call-done = f32[256,1536]{1,0:T(8,128)} async-done(((f32[1024,1536]{1,0:T(8,128)}), f32[256,1536]{1,0:T(8,128)}) %reduce-scatter.23.cloned.1.call-update) | async-done | bytes 1572880 | tf_op jit(solution)/shard_map/reduce_scatter | solution.py:44
  556.0 3.9 fusion.6
  560.0 62.1 %all-gather.6.cloned.1.call-done = bf16[1024,1536]{1,0:T(8,128)(2,1)} async-done(((bf16[256,1536]{1,0:T(8,128)(2,1)}), bf16[1024,1536]{1,0:T(8,128)(2,1)}) %all-gather.6.cloned.1.call-update) | async-done | bytes 3145744 | tf_op jit(solution)/shard_map/all_gather | solution.py:20
  622.1 4.1 fusion.39
  626.2 17.6 %reduce-scatter.25.cloned.1.call-done = f32[512,192]{0,1:T(8,128)} async-done(((f32[1024,192]{0,1:T(8,128)}), f32[512,192]{0,1:T(8,128)}) %reduce-scatter.25.cloned.1.call-update) | async-done | bytes 393232 | tf_op jit(solution)/shard_map/reduce_scatter | solution.py:50
  643.8 2.7 multiply_reduce_fusion.1
  646.5 7.0 all-reduce.1
  654.7 5.2 all_gather.38
  661.5 37.8 %reduce-scatter.27.cloned.1.call-done = f32[256,384]{1,0:T(8,128)} async-done(((f32[1024,384]{1,0:T(8,128)}), f32[256,384]{1,0:T(8,128)}) %reduce-scatter.27.cloned.1.call-update) | async-done | bytes 393232 | tf_op jit(solution)/shard_map/reduce_scatter | solution.py:44
  701.0 4.1 all-to-all-start.2
  706.0 2.8 all-to-all-done.2
  710.6 2.1 convolution_convert_fusion
  712.8 1.8 multiply_reduce_fusion
  719.4 3.6 all-to-all-start.3
  723.1 3.2 reduce-scatter.33.cloned.1.call-done
  727.3 15.0 %reduce-scatter.31.cloned.1.call-done = bf16[384,256]{1,0:T(8,128)(2,1)} async-done(((bf16[768,256]{1,0:T(8,128)(2,1)}), bf16[384,256]{1,0:T(8,128)(2,1)}) %reduce-scatter.31.cloned.1.call-update) | async-done | bytes 196624
  744.3 48.9 %all-gather.8.cloned.1.call-done = bf16[1024,1152]{1,0:T(8,128)(2,1)} async-done(((bf16[256,1152]{1,0:T(8,128)(2,1)}), bf16[1024,1152]{1,0:T(8,128)(2,1)}) %all-gather.8.cloned.1.call-update) | async-done | bytes 2359312 | tf_op jit(solution)/shard_map/all_gather | solution.py:20
  793.2 3.5 fusion.41
  796.8 3.8 fusion.44
  805.6 2.4 convert_reduce_fusion
  808.0 14.6 %all-reduce = (f32[192]{0:T(256)}, f32[192]{0:T(256)}, f32[192]{0:T(256)}, f32[192]{0:T(256)}) all-reduce(f32[192]{0:T(256)S(1)} %copy-done.38, f32[192]{0:T(256)S(1)} %copy-done.39, f32[192]{0:T(256)S(1)} %copy-done.40, f32[192]{0:T(256)S(1)} %convert_reduce_fusion.5), channel_id=1, replica_groups=mesh['dp'=4,'row'=4,'col'=2] {'dp','col'}, use_global_device_ids=true, to_apply=%region_38.39 | all-reduce | flops 768 | bytes 6144 | tf_op jit(solution)/shard_map/psum | solution.py:244
  824.5 11.5 %all-reduce.3 = (f32[384]{0:T(512)}, f32[384]{0:T(512)}, f32[192]{0:T(256)}, f32[1536]{0:T(1024)}, f32[192]{0:T(256)}) all-reduce(f32[384]{0:T(512)S(1)} %get-tuple-element.18, f32[384]{0:T(512)S(1)} %get-tuple-element.17, f32[192]{0:T(256)S(1)} %convert_reduce_fusion.4, ...), channel_id=1, replica_groups=mesh['dp'=4,'row'=4,'col'=2] {'dp'}, use_global_device_ids=true, to_apply=%region_31.32 | all-reduce | flops 2688 | bytes 21504 | tf_op jit(solution)/shard_map/psum | solution.py:230
  836.0 1.9 add_bitcast_fusion
  837.9 55.4 %all-reduce.7.cloned.1.call-done = (f32[192,1152]{1,0:T(8,128)}, f32[384,192]{0,1:T(8,128)}, f32[192,1536]{1,0:T(8,128)}, f32[1536,192]{0,1:T(8,128)}) async-done(((f32[192,1152]{1,0:T(8,128)}, f32[384,192]{0,1:T(8,128)}, f32[192,1536]{1,0:T(8,128)}, f32[1536,192]{0,1:T(8,128)}), (f32[192,1152]{1,0:T(8,128)}, f32[384,192]{0,1:T(8,128)}, f32[192,1536]{1,0:T(8,128)}, ...) | async-done | bytes 3538960 | tf_op jit(solution)/shard_map/psum | solution.py:230
  893.3 2.2 fusion.33
  (176 shorter events, 40.8 us)
Async XLA Ops:
  7.2 375.2 %copy-start = (bf16[1536,192]{0,1:T(8,128)(2,1)S(1)}, bf16[1536,192]{0,1:T(8,128)(2,1)}, u32[]{:S(2)}) copy-start(bf16[1536,192]{0,1:T(8,128)(2,1)} %param.31) | copy-start | bytes 1769476
  7.2 100.6 %reduce-scatter.15.cloned.1.call-start = ((), (), s32[]{:S(2)}) async-start(), calls=%async_computation.14 | async-start | bytes 5898240 | tf_op jit(solution)/shard_map/reduce_scatter | solution.py:44
  14.0 5.9 copy-start.8
  17.0 3.0 copy-start.10
  19.9 87.9 %copy-start.43 = (f32[384]{0:T(512)S(1)}, f32[384]{0:T(512)}, u32[]{:S(2)}) copy-start(f32[384]{0:T(512)} %param.23) | copy-start | bytes 4612
  20.0 87.9 %copy-start.44 = (f32[384]{0:T(512)S(1)}, f32[384]{0:T(512)}, u32[]{:S(2)}) copy-start(f32[384]{0:T(512)} %param.24) | copy-start | bytes 4612
  109.8 18.1 %all-to-all-start = ((bf16[2,128,384]{1,2,0:T(8,128)(2,1)}), bf16[2,128,384]{1,2,0:T(8,128)(2,1)S(1)}, u32[]{:S(2)}, u32[]{:S(2)}) async-start(bf16[2,128,384]{1,2,0:T(8,128)(2,1)} %bitcast.125), calls=%async_computation.1 | async-start | bytes 393216 | tf_op jit(solution)/shard_map/all_to_all | solution.py:36
  113.3 61.7 %reduce-scatter.17.cloned.1.call-start = ((), (), s32[]{:S(2)}) async-start(), calls=%async_computation.15 | async-start | bytes 1179648 | tf_op jit(solution)/shard_map/reduce_scatter | solution.py:50
  121.9 7.1 copy-start.13
  129.7 22.0 %copy-start.22 = (bf16[384,192]{0,1:T(8,128)(2,1)S(1)}, bf16[384,192]{0,1:T(8,128)(2,1)}, u32[]{:S(2)}) copy-start(bf16[384,192]{0,1:T(8,128)(2,1)} %param.25) | copy-start | bytes 442372
  136.0 39.0 %copy-start.21 = (bf16[192,512]{1,0:T(8,128)(2,1)S(1)}, bf16[192,512]{1,0:T(8,128)(2,1)}, u32[]{:S(2)}) copy-start(bf16[192,512]{1,0:T(8,128)(2,1)} %param.18) | copy-start | bytes 589828
  136.0 39.0 %copy-start.45 = (f32[192]{0:T(256)S(1)}, f32[192]{0:T(256)}, u32[]{:S(2)}) copy-start(f32[192]{0:T(256)} %param.26) | copy-start | bytes 2308
  151.7 38.6 %copy-start.29 = (f32[192]{0:T(256)S(1)}, f32[192]{0:T(256)}, u32[]{:S(2)}) copy-start(f32[192]{0:T(256)} %param.27) | copy-start | bytes 2308
  151.7 38.6 %copy-start.41 = (f32[192]{0:T(256)S(1)}, f32[192]{0:T(256)}, u32[]{:S(2)}) copy-start(f32[192]{0:T(256)} %param.28) | copy-start | bytes 2308
  153.1 43.4 %copy-start.24 = (bf16[192,1536]{1,0:T(8,128)(2,1)S(1)}, bf16[192,1536]{1,0:T(8,128)(2,1)}, u32[]{:S(2)}) copy-start(bf16[192,1536]{1,0:T(8,128)(2,1)} %param.29) | copy-start | bytes 1769476
  153.1 164.3 %reduce-scatter.19.cloned.1.call-start = ((), (), s32[]{:S(2)}) async-start(), calls=%async_computation.16 | async-start | bytes 7864320 | tf_op jit(solution)/shard_map/reduce_scatter | solution.py:44
  200.1 117.3 %copy-start.27 = (f32[1536]{0:T(1024)S(1)}, f32[1536]{0:T(1024)}, u32[]{:S(2)}) copy-start(f32[1536]{0:T(1024)} %param.30) | copy-start | bytes 18436
  200.2 182.3 %all-gather.4.cloned.1.call-start = ((), (), s32[]{:S(2)}) async-start(), calls=%async_computation.17 | async-start | bytes 3932160 | tf_op jit(solution)/shard_map/all_gather | solution.py:20
  320.3 83.8 %copy-start.42 = (f32[192]{0:T(256)S(1)}, f32[192]{0:T(256)}, u32[]{:S(2)}) copy-start(f32[192]{0:T(256)} %param.28) | copy-start | bytes 2308
  320.3 83.7 %copy-start.47 = (f32[192]{0:T(256)S(1)}, f32[192]{0:T(256)}, u32[]{:S(2)}) copy-start(f32[192]{0:T(256)} %param.32) | copy-start | bytes 2308
  320.3 83.7 %reduce-scatter.21.cloned.1.call-start = ((), (), s32[]{:S(2)}) async-start(), calls=%async_computation.18 | async-start | bytes 1179648 | tf_op jit(solution)/shard_map/reduce_scatter | solution.py:50
  386.4 33.2 %copy-start.15 = (bf16[192,512]{1,0:T(8,128)(2,1)S(1)}, bf16[192,512]{1,0:T(8,128)(2,1)}, u32[]{:S(2)}) copy-start(bf16[192,512]{1,0:T(8,128)(2,1)} %param.35) | copy-start | bytes 589828
  386.4 33.2 %copy-start.37 = (f32[192]{0:T(256)S(1)}, f32[192]{0:T(256)}, u32[]{:S(2)}) copy-start(f32[192]{0:T(256)} %param.33) | copy-start | bytes 2308
  386.4 169.6 %reduce-scatter.23.cloned.1.call-start = ((), (), s32[]{:S(2)}) async-start(), calls=%async_computation.19 | async-start | bytes 7864320 | tf_op jit(solution)/shard_map/reduce_scatter | solution.py:44
  437.8 184.3 %all-gather.6.cloned.1.call-start = ((), (), s32[]{:S(2)}) async-start(), calls=%async_computation.20 | async-start | bytes 3932160 | tf_op jit(solution)/shard_map/all_gather | solution.py:20
  559.9 83.9 %reduce-scatter.25.cloned.1.call-start = ((), (), s32[]{:S(2)}) async-start(), calls=%async_computation.21 | async-start | bytes 1179648 | tf_op jit(solution)/shard_map/reduce_scatter | solution.py:50
  626.1 73.2 %reduce-scatter.27.cloned.1.call-start = ((), (), s32[]{:S(2)}) async-start(), calls=%async_computation.22 | async-start | bytes 1966080 | tf_op jit(solution)/shard_map/reduce_scatter | solution.py:44
  653.5 6.4 copy-start.23
  653.5 8.0 copy-start.31
  653.5 8.0 copy-start.33
  701.0 7.8 all-to-all-start.2
  705.1 21.1 %reduce-scatter.33.cloned.1.call-start = ((), (), s32[]{:S(2)}) async-start(), calls=%async_computation.26 | async-start | bytes 589824
  712.8 29.5 %reduce-scatter.31.cloned.1.call-start = ((), (), s32[]{:S(2)}) async-start(), calls=%async_computation.25 | async-start | bytes 589824
  719.4 73.8 %copy-start.11 = (bf16[192,1152]{1,0:T(8,128)(2,1)S(1)}, bf16[192,1152]{1,0:T(8,128)(2,1)}, u32[]{:S(2)}) copy-start(bf16[192,1152]{1,0:T(8,128)(2,1)} %copy-done.10) | copy-start | bytes 1327108
  719.4 23.9 %all-to-all-start.3 = ((bf16[128,2,384]{2,0,1:T(8,128)(2,1)}), bf16[128,2,384]{2,0,1:T(8,128)(2,1)S(1)}, u32[]{:S(2)}, u32[]{:S(2)}) async-start(bf16[128,2,384]{2,0,1:T(8,128)(2,1)} %copy.46), calls=%async_computation.10 | async-start | bytes 393216 | tf_op jit(solution)/shard_map/all_to_all | solution.py:40
  723.0 70.2 %all-gather.8.cloned.1.call-start = ((), (), s32[]{:S(2)}) async-start(), calls=%async_computation.23 | async-start | bytes 2949120 | tf_op jit(solution)/shard_map/all_gather | solution.py:20
  744.3 91.7 %reduce-scatter.29.cloned.1.call-start = ((), (), s32[]{:S(2)}) async-start(), calls=%async_computation.24 | async-start | bytes 1179648 | tf_op jit(solution)/shard_map/reduce_scatter | solution.py:50
  796.7 3.9 copy-start.7
  796.7 96.5 %all-reduce.7.cloned.1.call-start = ((), (), s32[]{:S(2)}) async-start(), calls=%async_computation.27 | async-start | bytes 7077888 | tf_op jit(solution)/shard_map/psum | solution.py:230
  796.8 3.8 copy-start.2
  800.6 2.9 copy-start.1
  805.5 2.5 copy-start.39
  805.5 2.5 copy-start.40
  808.0 28.0 %copy-start.12 = (f32[512,192]{0,1:T(8,128)S(1)}, f32[512,192]{0,1:T(8,128)}, u32[]{:S(2)}) copy-start(f32[512,192]{0,1:T(8,128)} %get-tuple-element.43) | copy-start | bytes 1179652
  808.0 28.0 %copy-start.30 = (f32[192]{0:T(256)S(1)}, f32[192]{0:T(256)}, u32[]{:S(2)}) copy-start(f32[192]{0:T(256)} %param.27) | copy-start | bytes 2308
  808.0 28.0 %copy-start.32 = (f32[512,1]{0,1:T(1,128)S(1)}, f32[512,1]{0,1:T(1,128)}, u32[]{:S(2)}) copy-start(f32[512,1]{0,1:T(1,128)} %copy-done.31) | copy-start | bytes 6148
  808.0 28.0 %copy-start.34 = (f32[512,1]{0,1:T(1,128)S(1)}, f32[512,1]{0,1:T(1,128)}, u32[]{:S(2)}) copy-start(f32[512,1]{0,1:T(1,128)} %copy-done.33) | copy-start | bytes 6148
  893.3 2.9 copy-start.20
  (17 other events, 20.4 us)
Sparse Core Ops, SparseCore 0:
  20.1 87.6 reduce-scatter.14
  153.2 21.6 reduce-scatter.16
  200.3 117.0 reduce-scatter.18
  320.4 61.9 all-gather.3
  386.5 17.4 reduce-scatter.20
  437.9 118.0 reduce-scatter.22
  560.0 61.9 all-gather.5
  626.3 17.4 reduce-scatter.24
  661.7 37.6 reduce-scatter.26
  712.9 13.3 reduce-scatter.32
  728.5 13.7 reduce-scatter.30
  744.4 48.7 all-gather.7
  796.8 17.4 reduce-scatter.28
  818.0 75.2 all-reduce.6
where the time goes:
time: 908 us; the launch traced here: 905 us
  waiting for transfers between devices  667 us (73%)
  blocking collectives  126 us (14%)
  matrix products  40.8 us (4%)
  other arithmetic  26 us (3%)
  local copies, waits for them, and re-layouts  18.4 us (2%)
  between operations  14.4 us (2%)
  starting transfers between devices  11.8 us (1%)
    reduce_scatter x4, waiting for transfers between devices, sum_over_row(): lax.psum_scatter(product_rows(gathered, block, flipped), 'row', scatter_d...  360 us
    all_gather x3, waiting for transfers between devices, gather_over_row(): return lax.all_gather(values, 'row', axis=0, tiled=True)  173 us
    reduce_scatter x4, waiting for transfers between devices, sum_over_col(): lax.psum_scatter(product_rows(gathered, block, flipped), 'col', scatter_d...  57 us
    psum x1, waiting for transfers between devices, body(): lax.psum((joined_weight_grad, query_bias_grad, value_bias_grad, out_weigh...  55.4 us
    psum x6, blocking collectives, row_totals(): return lax.psum(values, 'row')  43.1 us
    all_gather x4, blocking collectives, gather_over_col(): return lax.all_gather(values, 'col', axis=0, tiled=True)  22.6 us
    unnamed x16, waiting for transfers between devices  18.4 us
  transfers between devices with their start and end apart: 17, of which 14 were waited for; matrix products, arithmetic and copies ran while one was open for 3% of the time, Pallas kernels for 0%

commit v1 on v0

--- a/solution.py
+++ b/solution.py
@@ -3,6 +3,8 @@
 import jax
 import jax.numpy as jnp
 from jax import lax
+from jax.experimental import pallas as pl
+from jax.experimental.pallas import tpu as pltpu
 from jax.sharding import PartitionSpec as P
 
 HEADS = 12
@@ -265,6 +267,925 @@
     )
 
 
+MESH_ID = pl.DeviceIdType.MESH
+BF = jnp.bfloat16
+F32 = jnp.float32
+GRID = {"dp": 4, "row": 4, "col": 2}
+SEQ = 256
+WIDE = 768
+HALF = 128
+ROWS = 192
+CHUNK = 384
+CHUNKS = 12
+SEMS = 256
+
+
+def small_grid(mesh):
+    return dict(mesh.shape) == GRID
+
+
+def mm(a, b):
+    return jnp.dot(a, b, preferred_element_type=F32)
+
+
+def mm_nt(a, b):
+    return lax.dot_general(a, b, (((1,), (1,)), ((), ())), preferred_element_type=F32)
+
+
+def loop(count, step):
+    def wrapped(i, carry):
+        step(i)
+        return carry
+
+    lax.fori_loop(0, count, wrapped, 0)
+
+
+def row_mean(values):
+    return jnp.sum(values, axis=1, keepdims=True) * (1.0 / WIDE)
+
+
+def fold(values):
+    return jnp.sum(values.reshape(values.shape[0] // 8, 8, values.shape[1]), axis=0)
+
+
+def layer_kernel(
+    ids,
+    tok,
+    cot,
+    qw,
+    kw,
+    vw,
+    ow,
+    uw,
+    dw,
+    qb,
+    vb,
+    ub,
+    own_vec,
+    fin_out,
+    res_out,
+    tg_out,
+    vec_out,
+    W,
+    G,
+    R1,
+    R2,
+    RD,
+    RU,
+    fin,
+    xin,
+    cin,
+    xs,
+    xr,
+    vg,
+    vec,
+    VA,
+    VB,
+    VC,
+    VD,
+    VZ,
+    xf,
+    cf,
+    neq,
+    q,
+    k,
+    v,
+    qT,
+    kT,
+    P,
+    at,
+    hid,
+    n1,
+    s1,
+    hb,
+    hT,
+    act,
+    dact,
+    outf,
+    r2g,
+    dg,
+    dgT,
+    pg,
+    fg,
+    fgT,
+    pgT,
+    prg,
+    dA,
+    dAT,
+    dT,
+    tgp,
+    tgr,
+    osend,
+    obuf,
+    tsend,
+    tbuf,
+    send,
+    recv,
+):
+    dp = lax.axis_index("dp")
+    z = lax.axis_index("row")
+    x = lax.axis_index("col")
+    core = lax.rem(dp, 2)
+    y = lax.div(dp, 2)
+    mate = dp + 1 - 2 * core
+    far = lax.rem(dp + 2, 4)
+    matefar = lax.rem(mate + 2, 4)
+    other = 1 - x
+    counts = {"s": 0, "r": 0}
+    pending = []
+
+    def new(kind, n=1):
+        base = counts[kind]
+        counts[kind] = base + n
+        assert counts[kind] <= SEMS
+        return base
+
+    def push(src, dst, ssem, rsem, **where):
+        return pltpu.make_async_remote_copy(
+            src_ref=src,
+            dst_ref=dst,
+            send_sem=send.at[ssem],
+            recv_sem=recv.at[rsem],
+            device_id=where,
+            device_id_type=MESH_ID,
+        )
+
+    def start(pred, make):
+        if pred is None:
+            make().start()
+        else:
+
+            @pl.when(pred)
+            def _():
+                make().start()
+
+        pending.append((pred, make))
+
+    def arrived(dst, rsem, **where):
+        push(dst, dst, 0, rsem, **where).wait_recv()
+
+    def rows(b):
+        return pl.ds(pl.multiple_of(b * ROWS, ROWS), ROWS)
+
+    bar = pltpu.get_barrier_semaphore()
+    for j in range(4):
+        for h in range(2):
+
+            @pl.when((z != j) | (x != h))
+            def _(j=j, h=h):
+                pl.semaphore_signal(bar, inc=1, device_id={"row": j, "col": h}, device_id_type=MESH_ID)
+
+    pl.semaphore_signal(bar, inc=1, device_id={"dp": mate}, device_id_type=MESH_ID)
+    pl.semaphore_signal(bar, inc=1, device_id={"dp": far}, device_id_type=MESH_ID)
+
+    lsem = new("s", CHUNKS)
+    mine = rows(z)
+
+    def local_parts():
+        parts = []
+        for j, ref in enumerate((qw, kw, vw, ow)):
+            parts.append((ref, W.at[j, mine]))
+        for i in range(4):
+            parts.append((uw.at[:, i * CHUNK : (i + 1) * CHUNK], W.at[4 + i, mine]))
+        for i in range(4):
+            parts.append((dw.at[:, i * CHUNK : (i + 1) * CHUNK], W.at[8 + i, mine]))
+        return [pltpu.make_async_copy(a, b, send.at[lsem + n]) for n, (a, b) in enumerate(parts)]
+
+    locals_ = local_parts()
+    for c in locals_:
+        c.start()
+    vg[z] = own_vec[...]
+    seg = jnp.broadcast_to(ids[...].astype(F32), (SEQ, SEQ))
+    neq[...] = jnp.abs(seg - seg.T)
+    pl.semaphore_wait(bar, 9)
+
+    def spread(ref, landing):
+        ssem, rsem = new("s", 4), new("r", 4)
+        for s in range(2):
+            for h in range(2):
+                jj = 2 * x + s
+                self_ = (jj == z) & (h == x)
+                src = ref.at[:, s * SEQ + h * HALF : s * SEQ + (h + 1) * HALF]
+                dst = landing.at[h, mine]
+                start(
+                    jnp.logical_not(self_),
+                    lambda src=src, dst=dst, n=2 * s + h, jj=jj, h=h: push(
+                        src, dst, ssem + n, rsem + z, row=jj, col=h
+                    ),
+                )
+
+                @pl.when(self_)
+                def _(src=src, dst=dst):
+                    pltpu.make_async_copy(src, dst, recv.at[rsem + z]).start()
+
+        def collect():
+            home = lax.div(z, 2) == x
+            for b in range(4):
+                local = home & (z == b)
+                dst = landing.at[x, rows(b)]
+
+                @pl.when(local)
+                def _(dst=dst, b=b):
+                    pltpu.make_async_copy(ref.at[:, 0:HALF], dst, recv.at[rsem + b]).wait()
+
+                @pl.when(jnp.logical_not(local))
+                def _(dst=dst, b=b):
+                    arrived(dst, rsem + b, col=other)
+
+        return collect
+
+    def swap(landing):
+        ssem, rsem = new("s"), new("r")
+        start(None, lambda: push(landing.at[x], landing.at[x], ssem, rsem, col=other))
+
+        def collect():
+            arrived(landing.at[other], rsem, col=other)
+
+        return collect
+
+    def share_vec():
+        ssem, rsem = new("s", 3), new("r", 4)
+        for o in range(1, 4):
+            to = lax.rem(z + o, 4)
+            start(None, lambda o=o, to=to: push(own_vec, vg.at[z], ssem + o - 1, rsem + z, row=to))
+
+        def collect():
+            for o in range(1, 4):
+                b = lax.rem(z + o, 4)
+                arrived(vg.at[b], rsem + b, row=b)
+            vec[...] = vg[0] + vg[1] + vg[2] + vg[3]
+
+        return collect
+
+    def gather(g):
+        zs, ys, cs = new("s", 6), new("s", 4), new("s", 8)
+        zr, yr, cr = new("r", 4), new("r", 4), new("r", 8)
+        own, ychunk = 4 * g + dp, 4 * g + far
+
+        def block(chunk, b):
+            return W.at[chunk, rows(b)]
+
+        def up(d, b, pred):
+            start(pred, lambda: push(block(own, b), block(own, b), zs + d, zr + b, row=z + 1))
+
+        def down(d, b, pred):
+            start(pred, lambda: push(block(own, b), block(own, b), zs + 3 + d, zr + b, row=z - 1))
+
+        def first():
+            up(0, z, z < 3)
+            down(0, z, z > 0)
+
+        def hop(d):
+            for below in (True, False):
+                b = z - d if below else z + d
+                here = z >= d if below else z + d <= 3
+
+                @pl.when(here)
+                def _(b=b):
+                    arrived(block(own, b), zr + b, row=b)
+
+                if d < 3:
+                    if below:
+                        up(d, b, here & (z < 3))
+                    else:
+                        down(d, b, here & (z > 0))
+                start(here, lambda b=b: push(block(own, b), block(own, b), ys + b, yr + b, dp=far))
+                start(here, lambda b=b: push(block(own, b), block(own, b), cs + b, cr + b, dp=mate))
+
+        def across():
+            for b in range(4):
+                there = z != b
+
+                @pl.when(there)
+                def _(b=b):
+                    arrived(block(ychunk, b), yr + b, dp=far)
+
+                start(
+                    there,
+                    lambda b=b: push(block(ychunk, b), block(ychunk, b), cs + 4 + b, cr + 4 + b, dp=mate),
+                )
+
+        def finish():
+            for b in range(4):
+
+                @pl.when(z != b)
+                def _(b=b):
+                    arrived(block(4 * g + mate, b), cr + b, dp=mate)
+                    arrived(block(4 * g + matefar, b), cr + 4 + b, dp=mate)
+
+        return first, hop, across, finish
+
+    def exchange(n):
+        ssem, rsem = new("s", 3), new("r", 3)
+
+        def put(c, value):
+            xs[n, c] = value.astype(BF)
+            start(None, lambda: push(xs.at[n, c], xr.at[n, c], ssem + c, rsem + c, col=other))
+
+        def collect():
+            for c in range(3):
+                arrived(xr.at[n, c], rsem + c, col=other)
+
+        return put, collect
+
+    def both(n, r):
+        own = [xs[n, c, r, :].astype(F32) + xr[n, c, r, :].astype(F32) for c in range(3)]
+        return jnp.concatenate(own, axis=1)
+
+    def reduce(g):
+        s1_, s2_, sd, su, sy, sc = new("s", 2), new("s"), new("s", 3), new("s", 3), new("s"), new("s", 2)
+        r1, r2, rd, ru, ry, rc = new("r", 2), new("r"), new("r", 3), new("r", 3), new("r"), new("r", 2)
+        own, ychunk = 4 * g + dp, 4 * g + far
+        sf = new("s", 2)
+
+        def to_core():
+            for j in range(2):
+                src = G.at[4 * g + 2 * j + 1 - core]
+                start(None, lambda src=src, j=j: push(src, R1.at[g, j], s1_ + j, r1 + j, dp=mate))
+
+        def add(chunk, extra, base, count):
+            def step(i):
+                at_ = pl.ds(pl.multiple_of(base + i * 64, 64), 64)
+                from_ = pl.ds(pl.multiple_of(i * 64, 64), 64)
+                G[chunk, at_, :] = (G[chunk, at_, :].astype(F32) + extra[from_, :].astype(F32)).astype(BF)
+
+            loop(count // 64, step)
+
+        def to_y():
+            for j in (1 - y, y):
+                chunk = 4 * g + 2 * j + core
+                arrived(R1.at[g, j], r1 + j, dp=mate)
+                add(chunk, R1.at[g, j], 0, WIDE)
+                if j is not y:
+                    start(None, lambda: push(G.at[ychunk], R2.at[g], s2_, r2, dp=far))
+
+        def piece(b):
+            return G.at[own, rows(b)]
+
+        def send_down(b, pred):
+            start(pred, lambda: push(piece(b), RD.at[g, b], sd + b, rd + b, row=z - 1))
+
+        def send_up(b, pred):
+            start(pred, lambda: push(piece(b), RU.at[g, b - 1], su + b - 1, ru + b - 1, row=z + 1))
+
+        def take_down(b):
+            arrived(RD.at[g, b], rd + b, row=z + 1)
+            add(own, RD.at[g, b], b * ROWS, ROWS)
+
+        def take_up(b):
+            arrived(RU.at[g, b - 1], ru + b - 1, row=z - 1)
+            add(own, RU.at[g, b - 1], b * ROWS, ROWS)
+
+        def chain0():
+            arrived(R2.at[g], r2, dp=far)
+            add(own, R2.at[g], 0, WIDE)
+            for b in (0, 1, 2):
+                send_down(b, z == 3)
+            for b in (3, 2, 1):
+                send_up(b, z == 0)
+
+        def chain1():
+            for b in (0, 1):
+
+                @pl.when(z == 2)
+                def _(b=b):
+                    take_down(b)
+
+                send_down(b, z == 2)
+            for b in (3, 2):
+
+                @pl.when(z == 1)
+                def _(b=b):
+                    take_up(b)
+
+                send_up(b, z == 1)
+
+        def chain2():
+            @pl.when(z == 1)
+            def _():
+                take_down(0)
+
+            send_down(0, z == 1)
+
+            @pl.when(z == 2)
+            def _():
+                take_up(3)
+
+            send_up(3, z == 2)
+
+        def settle():
+            @pl.when(z < 3)
+            def _():
+                take_down(z)
+
+            @pl.when(z > 0)
+            def _():
+                take_up(z)
+
+            fin[own] = G[own, mine, :]
+            start(None, lambda: push(fin.at[own], fin.at[own], sy, ry, dp=far))
+            start(None, lambda: push(fin.at[own], fin.at[own], sc, rc, dp=mate))
+
+        def across():
+            arrived(fin.at[ychunk], ry, dp=far)
+            start(None, lambda: push(fin.at[ychunk], fin.at[ychunk], sc + 1, rc + 1, dp=mate))
+
+        def finish():
+            arrived(fin.at[4 * g + mate], rc, dp=mate)
+            arrived(fin.at[4 * g + matefar], rc + 1, dp=mate)
+
+        return to_core, to_y, chain0, chain1, chain2, settle, across, finish
+
+    def deliver(sent, landed, out):
+        ssem, rsem = new("s", 4), new("r", 4)
+        slot = 2 * lax.rem(z, 2) + x
+        home = lax.div(z, 2) == x
+        for b in range(4):
+            self_ = home & (z == b)
+            start(
+                jnp.logical_not(self_),
+                lambda b=b: push(
+                    sent.at[rows(b)], landed.at[slot], ssem + b, rsem + slot, row=b, col=lax.div(z, 2)
+                ),
+            )
+
+            @pl.when(self_)
+            def _(b=b):
+                pltpu.make_async_copy(sent.at[rows(b)], landed.at[slot], recv.at[rsem + slot]).start()
+
+        def collect():
+            osem = new("s", 4)
+            copies = []
+            for n in range(4):
+                s, h = n // 2, n % 2
+                local = (2 * x + s == z) & (h == x)
+
+                @pl.when(local)
+                def _(n=n):
+                    pltpu.make_async_copy(sent.at[rows(z)], landed.at[n], recv.at[rsem + n]).wait()
+
+                @pl.when(jnp.logical_not(local))
+                def _(n=n):
+                    arrived(landed.at[n], rsem + n, col=other)
+
+                copies.append(
+                    pltpu.make_async_copy(
+                        landed.at[n], out.at[:, n * HALF : (n + 1) * HALF], send.at[osem + n]
+                    )
+                )
+                copies[-1].start()
+            return copies
+
+        return collect
+
+    tok_in = spread(tok, xin)
+    vec_in = share_vec()
+    gathers = [gather(g) for g in range(3)]
+    for c in locals_:
+        c.wait()
+    for g in range(3):
+        gathers[g][0]()
+    cot_in = spread(cot, cin)
+    tok_in()
+    tok_swap = swap(xin)
+    gathers[0][1](1)
+    gathers[0][1](2)
+    gathers[0][1](3)
+    tok_swap()
+    vec_in()
+    for h in range(2):
+        xf[h * HALF : (h + 1) * HALF, :] = xin[h].astype(F32).T
+    gathers[0][2]()
+    gathers[1][1](1)
+    gathers[1][1](2)
+    gathers[1][1](3)
+    gathers[0][3]()
+
+    xb = xf[...].astype(BF)
+    for j, (dst, bias) in enumerate(((q, qb), (k, None), (v, vb))):
+        r = mm(xb, W[j])
+        if bias is not None:
+            r = r + bias[...]
+        for p in range(3):
+            dst[p] = r[:, p * HALF : (p + 1) * HALF].astype(BF)
+
+    lane = lax.broadcasted_iota(jnp.int32, (SEQ, HALF), 1) < HEAD
+    scale = 1.0 / math.sqrt(HEAD)
+
+    def only(values, hh):
+        keep = lane if hh == 0 else jnp.logical_not(lane)
+        return jnp.where(keep, values.astype(F32), 0.0).astype(BF)
+
+    def attend(p):
+        qv, kv, vv = q[p], k[p], v[p]
+        outs = []
+        for hh in range(2):
+            s = mm_nt(only(qv, hh), kv) * scale
+            s = jnp.where(neq[...] == 0.0, s, -1000000000.0)
+            e = jnp.exp(s - jnp.max(s, axis=1, keepdims=True))
+            pr = e / jnp.sum(e, axis=1, keepdims=True)
+            P[2 * p + hh] = pr
+            outs.append(mm(pr.astype(BF), vv))
+        at[p] = jnp.where(lane, outs[0], outs[1]).astype(BF)
+
+    loop(3, attend)
+    gathers[2][1](1)
+
+    put0, get0 = exchange(0)
+    att = jnp.concatenate([at[0], at[1], at[2]], axis=1)
+    for c in range(3):
+        put0(c, mm_nt(att, W[3, c * SEQ : (c + 1) * SEQ, :]))
+    for p in range(3):
+        qT[p] = q[p].astype(F32).T.astype(BF)
+        kT[p] = k[p].astype(F32).T.astype(BF)
+    gathers[2][1](2)
+    gathers[2][1](3)
+    gathers[1][2]()
+    cot_in()
+    cot_swap = swap(cin)
+    get0()
+
+    def norm1(i):
+        r = pl.ds(pl.multiple_of(i * 32, 32), 32)
+        resid = xf[r, :] + (both(0, r) + vec[0:1, :])
+        d = resid - row_mean(resid)
+        s = lax.rsqrt(row_mean(d * d) + EPS)
+        n = d * s
+        h = n * vec[1:2, :] + vec[2:3, :]
+        n1[r, :] = n
+        s1[r, :] = jnp.broadcast_to(s, (32, HALF))
+        hid[r, :] = h
+        hb[r, :] = h.astype(BF)
+
+    loop(8, norm1)
+    gathers[1][3]()
+
+    hv = hb[...]
+    c0 = math.sqrt(2.0 / math.pi)
+
+    def up_step(i):
+        u = mm(hv, W[4 + i]) + ub[i]
+        u2 = u * u
+        t = jnp.tanh(c0 * (u + 0.044715 * (u2 * u)))
+        half = 0.5 * (1.0 + t)
+        act[i] = (u * half).astype(BF)
+        dact[i] = half + (0.5 * u) * (1.0 - t * t) * (c0 * (1.0 + (3 * 0.044715) * u2))
+
+    loop(4, up_step)
+    gathers[2][2]()
+    hT[...] = hid[...].T.astype(BF)
+    cot_swap()
+    for h in range(2):
+        cf[h * HALF : (h + 1) * HALF, :] = cin[h].astype(F32).T
+    gathers[2][3]()
+    put1, get1 = exchange(1)
+    for c in range(3):
+        acc = mm_nt(act[0], W[8, c * SEQ : (c + 1) * SEQ, :])
+        for i in range(1, 4):
+            acc = acc + mm_nt(act[i], W[8 + i, c * SEQ : (c + 1) * SEQ, :])
+        put1(c, acc)
+    get1()
+
+    VA[...] = jnp.zeros_like(VA)
+
+    def norm2(i, carry):
+        gain_sum, shift_sum, bias_sum = carry
+        r = pl.ds(pl.multiple_of(i * 32, 32), 32)
+        resid = hid[r, :] + (both(1, r) + vec[3:4, :])
+        d = resid - row_mean(resid)
+        s = lax.rsqrt(row_mean(d * d) + EPS)
+        n = d * s
+        outf[r, :] = n * vec[4:5, :] + vec[5:6, :]
+        up = cf[r, :]
+        e = up * vec[4:5, :]
+        grad = s * (e - row_mean(e) - n * row_mean(e * n))
+        low = grad.astype(BF)
+        r2g[r, :] = grad
+        dg[r, :] = low
+        return gain_sum + fold(up * n), shift_sum + fold(up), bias_sum + fold(low.astype(F32))
+
+    zero = jnp.zeros((8, WIDE), F32)
+    sums = lax.fori_loop(0, 8, norm2, (zero, zero, zero))
+
+    def total(values):
+        return jnp.sum(values, axis=0, keepdims=True)
+
+    VA[7:8, :] = total(sums[0])
+    VA[8:9, :] = total(sums[1])
+    VA[6:7, :] = total(sums[2])
+    dgT[...] = r2g[...].T.astype(BF)
+    reduces = [reduce(g) for g in range(3)]
+
+    def outer(dst, left, right):
+        def step(b):
+            r = pl.ds(pl.multiple_of(b * SEQ, SEQ), SEQ)
+            G[dst, r, :] = mm(left[r, :], right).astype(BF)
+
+        loop(3, step)
+
+    loop(4, lambda i: outer(8 + i, dgT, act[i]))
+    reduces[2][0]()
+
+    ones = jnp.ones((8, SEQ), BF)
+    dgv = dg[...]
+
+    def pre_step(i):
+        low = (mm(dgv, W[8 + i]) * dact[i]).astype(BF)
+        prg[i] = low
+
+    loop(4, pre_step)
+    put2, get2 = exchange(2)
+    for c in range(3):
+        acc = mm_nt(prg[0], W[4, c * SEQ : (c + 1) * SEQ, :])
+        for i in range(1, 4):
+            acc = acc + mm_nt(prg[i], W[4 + i, c * SEQ : (c + 1) * SEQ, :])
+        put2(c, acc)
+    for i in range(4):
+        VA[1 + i // 2 : 2 + i // 2, (i % 2) * CHUNK : (i % 2 + 1) * CHUNK] = mm(ones, prg[i])[0:1, :]
+    loop(4, lambda i: outer(4 + i, hT, prg[i]))
+    reduces[1][0]()
+    reduces[2][1]()
+
+    mine_tokens = pl.ds(pl.multiple_of(x * HALF, HALF), HALF)
+    osend[...] = outf[mine_tokens, :].T.astype(BF)
+    out_in = deliver(osend, obuf, res_out)
+    reduces[2][2]()
+    reduces[1][1]()
+    get2()
+
+    def norm1_back(i, carry):
+        gain_sum, shift_sum, bias_sum = carry
+        r = pl.ds(pl.multiple_of(i * 32, 32), 32)
+        up = r2g[r, :] + both(2, r)
+        n = n1[r, :]
+        s = s1[r, :][:, 0:1]
+        e = up * vec[1:2, :]
+        grad = s * (e - row_mean(e) - n * row_mean(e * n))
+        low = grad.astype(BF)
+        fg[r, :] = grad
+        pg[r, :] = low
+        return gain_sum + fold(up * n), shift_sum + fold(up), bias_sum + fold(low.astype(F32))
+
+    sums = lax.fori_loop(0, 8, norm1_back, (zero, zero, zero))
+    VA[4:5, :] = total(sums[0])
+    VA[5:6, :] = total(sums[1])
+    VA[3:4, :] = total(sums[2])
+    for h in range(2):
+        t = fg[h * HALF : (h + 1) * HALF, :].T
+        fgT[h] = t
+        pgT[:, h * HALF : (h + 1) * HALF] = t.astype(BF)
+
+    reduces[2][3]()
+    reduces[1][2]()
+    r = mm(pg[...], W[3])
+    for p in range(3):
+        part = r[:, p * HALF : (p + 1) * HALF].astype(BF)
+        dA[p] = part
+        dAT[p] = part.astype(F32).T.astype(BF)
+    outer(3, pgT, att)
+
+    top = lax.broadcasted_iota(jnp.int32, (HALF, SEQ), 0) < HEAD
+
+    def attend_back(p):
+        dAv, vv = dA[p], v[p]
+        dq, dk, dv = [], [], []
+        for hh in range(2):
+            pr = P[2 * p + hh]
+            pgrad = mm_nt(only(dAv, hh), vv)
+            ds = (pr * (pgrad - jnp.sum(pgrad * pr, axis=1, keepdims=True))).astype(BF)
+            dq.append(mm_nt(kT[p], ds))
+            dk.append(mm(qT[p], ds))
+            dv.append(mm(dAT[p], pr.astype(BF)))
+        dT[0, p] = (jnp.where(top, dq[0], dq[1]) * scale).astype(BF)
+        dT[1, p] = (jnp.where(top, dk[0], dk[1]) * scale).astype(BF)
+        dT[2, p] = jnp.where(top, dv[0], dv[1]).astype(BF)
+
+    loop(3, attend_back)
+    reduces[2][4]()
+    reduces[1][3]()
+
+    for j in range(3):
+        t = dT[j].reshape(CHUNK, SEQ)
+        if j != 1:
+            at_ = 0 if j == 0 else CHUNK
+            VA[0:1, at_ : at_ + CHUNK] = mm_nt(ones, t)[0:1, :]
+
+        def step(b, t=t, j=j):
+            r = pl.ds(pl.multiple_of(b * SEQ, SEQ), SEQ)
+            left = jnp.concatenate([xin[0, r, :], xin[1, r, :]], axis=1)
+            G[j, r, :] = mm_nt(left, t).astype(BF)
+
+        loop(3, step)
+    reduces[0][0]()
+    vs, vr = new("s", 5), new("r", 6)
+    start(None, lambda: push(VA, VB, vs, vr, dp=mate))
+
+    def back_step(b):
+        r = pl.ds(pl.multiple_of(b * SEQ, SEQ), SEQ)
+        acc = mm(W[0, r, :], dT[0].reshape(CHUNK, SEQ))
+        acc = acc + mm(W[1, r, :], dT[1].reshape(CHUNK, SEQ))
+        acc = acc + mm(W[2, r, :], dT[2].reshape(CHUNK, SEQ))
+        tgp[0, r, :] = acc[:, :HALF].astype(BF)
+        tgp[1, r, :] = acc[:, HALF:].astype(BF)
+
+    loop(3, back_step)
+    ts, tr = new("s"), new("r")
+    start(None, lambda: push(tgp.at[other], tgr, ts, tr, col=other))
+    reduces[0][1]()
+    reduces[2][5]()
+    reduces[1][4]()
+    arrived(VB, vr, dp=mate)
+    VD[...] = VA[...] + VB[...]
+    start(None, lambda: push(VD, VC, vs + 1, vr + 1, dp=far))
+    reduces[0][2]()
+    arrived(tgr, tr, col=other)
+    tsend[...] = (tgp[x].astype(F32) + tgr[...].astype(F32) + fgT[x]).astype(BF)
+    tg_in = deliver(tsend, tbuf, tg_out)
+    reduces[1][5]()
+    reduces[0][3]()
+    reduces[2][6]()
+    reduces[0][4]()
+    reduces[1][6]()
+    arrived(VC, vr + 1, dp=far)
+    VZ[z] = VD[...] + VC[...]
+    for o in range(1, 4):
+        to = lax.rem(z + o, 4)
+        start(None, lambda o=o, to=to: push(VZ.at[z], VZ.at[z], vs + 1 + o, vr + 2 + z, row=to))
+    reduces[0][5]()
+    reduces[2][7]()
+    reduces[1][7]()
+    copies = []
+    fsem = new("s", 3)
+
+    def flush(g):
+        c = pltpu.make_async_copy(
+            fin.at[4 * g : 4 * g + 4], fin_out.at[4 * g : 4 * g + 4], send.at[fsem + g]
+        )
+        c.start()
+        copies.append(c)
+
+    flush(2)
+    flush(1)
+    for o in range(1, 4):
+        b = lax.rem(z + o, 4)
+        arrived(VZ.at[b], vr + 2 + b, row=b)
+    vec_out[...] = VZ[0] + VZ[1] + VZ[2] + VZ[3]
+    copies += out_in()
+    copies += tg_in()
+    reduces[0][6]()
+    reduces[0][7]()
+    flush(0)
+    for pred, make in pending:
+        if pred is None:
+            make().wait_send()
+        else:
+
+            @pl.when(pred)
+            def _(make=make):
+                make().wait_send()
+
+    for c in copies:
+        c.wait()
+
+
+def fused_body(
+    tokens,
+    segment_ids,
+    query_weight,
+    key_weight,
+    value_weight,
+    query_bias,
+    value_bias,
+    out_weight,
+    out_bias,
+    attn_gain,
+    attn_shift,
+    up_weight,
+    up_bias,
+    down_weight,
+    down_bias,
+    ffn_gain,
+    ffn_shift,
+    cotangent,
+):
+    z = lax.axis_index("row")
+    vectors = jnp.stack([out_bias, attn_gain, attn_shift, down_bias, ffn_gain, ffn_shift])
+    vectors = jnp.pad(vectors, ((0, 2), (0, 0)))
+    placed = jnp.concatenate(
+        [jnp.where(z == b, vectors, 0.0) for b in range(4)], axis=1
+    )
+    hbm = pl.BlockSpec(memory_space=pl.ANY)
+    vmem = pl.BlockSpec(memory_space=pltpu.VMEM)
+    grads, out, tgrad, sums = pl.pallas_call(
+        layer_kernel,
+        out_shape=(
+            jax.ShapeDtypeStruct((CHUNKS, ROWS, CHUNK), BF),
+            jax.ShapeDtypeStruct((ROWS, 2 * SEQ), BF),
+            jax.ShapeDtypeStruct((ROWS, 2 * SEQ), BF),
+            jax.ShapeDtypeStruct((16, WIDE), F32),
+        ),
+        in_specs=[vmem] + [hbm] * 8 + [vmem] * 4,
+        out_specs=(hbm, hbm, hbm, vmem),
+        scratch_shapes=[
+            pltpu.VMEM((CHUNKS, WIDE, CHUNK), BF),
+            pltpu.VMEM((CHUNKS, WIDE, CHUNK), BF),
+            pltpu.VMEM((3, 2, WIDE, CHUNK), BF),
+            pltpu.VMEM((3, WIDE, CHUNK), BF),
+            pltpu.VMEM((3, 3, ROWS, CHUNK), BF),
+            pltpu.VMEM((3, 3, ROWS, CHUNK), BF),
+            pltpu.VMEM((CHUNKS, ROWS, CHUNK), BF),
+            pltpu.VMEM((2, WIDE, HALF), BF),
+            pltpu.VMEM((2, WIDE, HALF), BF),
+            pltpu.VMEM((3, 3, SEQ, SEQ), BF),
+            pltpu.VMEM((3, 3, SEQ, SEQ), BF),
+            pltpu.VMEM((4, 8, WIDE), F32),
+            pltpu.VMEM((8, WIDE), F32),
+            pltpu.VMEM((16, WIDE), F32),
+            pltpu.VMEM((16, WIDE), F32),
+            pltpu.VMEM((16, WIDE), F32),
+            pltpu.VMEM((16, WIDE), F32),
+            pltpu.VMEM((4, 16, WIDE), F32),
+            pltpu.VMEM((SEQ, WIDE), F32),
+            pltpu.VMEM((SEQ, WIDE), F32),
+            pltpu.VMEM((SEQ, SEQ), F32),
+            pltpu.VMEM((3, SEQ, HALF), BF),
+            pltpu.VMEM((3, SEQ, HALF), BF),
+            pltpu.VMEM((3, SEQ, HALF), BF),
+            pltpu.VMEM((3, HALF, SEQ), BF),
+            pltpu.VMEM((3, HALF, SEQ), BF),
+            pltpu.VMEM((6, SEQ, SEQ), F32),
+            pltpu.VMEM((3, SEQ, HALF), BF),
+            pltpu.VMEM((SEQ, WIDE), F32),
+            pltpu.VMEM((SEQ, WIDE), F32),
+            pltpu.VMEM((SEQ, HALF), F32),
+            pltpu.VMEM((SEQ, WIDE), BF),
+            pltpu.VMEM((WIDE, SEQ), BF),
+            pltpu.VMEM((4, SEQ, CHUNK), BF),
+            pltpu.VMEM((4, SEQ, CHUNK), F32),
+            pltpu.VMEM((SEQ, WIDE), F32),
+            pltpu.VMEM((SEQ, WIDE), F32),
+            pltpu.VMEM((SEQ, WIDE), BF),
+            pltpu.VMEM((WIDE, SEQ), BF),
+            pltpu.VMEM((SEQ, WIDE), BF),
+            pltpu.VMEM((SEQ, WIDE), F32),
+            pltpu.VMEM((2, WIDE, HALF), F32),
+            pltpu.VMEM((WIDE, SEQ), BF),
+            pltpu.VMEM((4, SEQ, CHUNK), BF),
+            pltpu.VMEM((3, SEQ, HALF), BF),
+            pltpu.VMEM((3, HALF, SEQ), BF),
+            pltpu.VMEM((3, 3, HALF, SEQ), BF),
+            pltpu.VMEM((2, WIDE, HALF), BF),
+            pltpu.VMEM((WIDE, HALF), BF),
+            pltpu.VMEM((WIDE, HALF), BF),
+            pltpu.VMEM((4, ROWS, HALF), BF),
+            pltpu.VMEM((WIDE, HALF), BF),
+            pltpu.VMEM((4, ROWS, HALF), BF),
+            pltpu.SemaphoreType.DMA((SEMS,)),
+            pltpu.SemaphoreType.DMA((SEMS,)),
+        ],
+        compiler_params=pltpu.CompilerParams(
+            collective_id=0, has_side_effects=True, vmem_limit_bytes=63 * 1024 * 1024
+        ),
+    )(
+        segment_ids,
+        tokens,
+        cotangent,
+        query_weight,
+        key_weight,
+        value_weight,
+        out_weight.T,
+        up_weight,
+        down_weight.T,
+        query_bias.reshape(1, CHUNK),
+        value_bias.reshape(1, CHUNK),
+        up_bias.reshape(4, 1, CHUNK),
+        placed,
+    )
+    wide = grads.astype(F32)
+    up_grad = wide[4:8].transpose(1, 0, 2).reshape(ROWS, 4 * CHUNK)
+    down_grad = wide[8:12].transpose(0, 2, 1).reshape(4 * CHUNK, ROWS)
+    slices = lax.dynamic_slice_in_dim(sums, z * ROWS, ROWS, 1)
+    return (
+        out,
+        tgrad.astype(F32),
+        wide[0],
+        wide[1],
+        wide[2],
+        sums[0, :CHUNK],
+        sums[0, CHUNK:],
+        wide[3].T,
+        slices[3],
+        slices[4],
+        slices[5],
+        up_grad,
+        sums[1:3].reshape(4 * CHUNK),
+        down_grad,
+        slices[6],
+        slices[7],
+        slices[8],
+    )
+
+
 def solution(mesh):
     placed = (
         P("row", ("dp", "col")),
@@ -287,7 +1208,7 @@
         P("row", ("dp", "col")),
     )
     return jax.shard_map(
-        body,
+        fused_body if small_grid(mesh) else body,
         mesh=mesh,
         in_specs=placed,
         out_specs=(

time: 908 us -> 195 us (0.21)
  waiting for transfers between devices: 667 us -> 0 us
  Pallas kernels: 0 us -> 175 us
  blocking collectives: 126 us -> 0 us
  matrix products: 40.8 us -> 0 us
  other arithmetic: 26 us -> 3.26 us
  between operations: 14.4 us -> 0.71 us
  starting transfers between devices: 11.8 us -> 0 us
    reduce_scatter x8 -> x0, waiting for transfers between devices: 417 us -> none  [the longest x4 360 us: sum_over_row(): lax.psum_scatter(product_rows(gathered, block, flipped), 'row', scatter_d...]
    pallas_call x0 -> x1, Pallas kernels: none -> 175 us  [fused_body(): pl.pallas_call(layer_kernel, out_shape=(jax.ShapeDtypeStruct((CHUNKS, ROW...]
    all_gather x3 -> x0, waiting for transfers between devices: 173 us -> none  [gather_over_row(): return lax.all_gather(values, 'row', axis=0, tiled=True)]
    psum x8 -> x0, blocking collectives: 69.2 us -> none  [the longest x6 43.1 us: row_totals(): return lax.psum(values, 'row')]
    psum x1 -> x0, waiting for transfers between devices: 55.4 us -> none  [body(): lax.psum((joined_weight_grad, query_bias_grad, value_bias_grad, out_weigh...]
    all_gather x7 -> x0, blocking collectives: 51 us -> none  [the longest x4 22.6 us: gather_over_col(): return lax.all_gather(values, 'col', axis=0, tiled=True)]
    dot_general x18 -> x0, matrix products: 40.8 us -> none  [the longest x4 12.9 us: contract(): lax.dot_general(left, weight, (((1,), (1,)), ((), ())), preferred_element...]
    unnamed x16 -> x0, waiting for transfers between devices: 18.4 us -> none
  transfers between devices with their start and end apart: 17 -> 0, of which waited for: 14 -> 0; matrix products, arithmetic and copies ran while one was open for 3% -> 0% of each run, Pallas kernels for 0% -> 0%
where the time goes in v1:
time: 195 us; the launch traced here: 192 us
  Pallas kernels  175 us (90%)
  local copies, waits for them, and re-layouts  13 us (7%)
  other arithmetic  3.26 us (2%)
    pallas_call x1, Pallas kernels, fused_body(): pl.pallas_call(layer_kernel, out_shape=(jax.ShapeDtypeStruct((CHUNKS, ROW...  175 us

profile of v1, /device:TPU:17, one launch (start us, length us, event | category | flops | bytes accessed | tf_op | source)
XLA Modules:
  0.0 192.3 jit_solution(4624253315663015542)
XLA Ops:
  0.7 0.8 stack.27
  1.5 0.7 pad_maximum_fusion.own_vec
  2.2 1.3 reshape.54.ub
  3.5 1.2 reshape.52.qb
  4.7 1.2 reshape.53.vb
  5.9 175.3 %shard_map.305 = (bf16[12,192,384]{2,1,0:T(8,128)(2,1)}, bf16[192,512]{1,0:T(8,128)(2,1)}, bf16[192,512]{1,0:T(8,128)(2,1)}, f32[16,768]{1,0:T(8,128)}) custom-call(s32[1,256]{1,0:T(1,128)} %ids.1, bf16[192,512]{1,0:T(8,128)(2,1)} %tok.1, bf16[192,512]{1,0:T(8,128)(2,1)} %cot.1, bf16[192,384]{1,0:T(8,128)(2,1)} %qw.1, bf16[192,384]{1,0:T(8,128)(2,1)} %kw.1, ...), custom_call_target="tpu_custom_call" | custom-call | tf_op jit(solution)/shard_map/pallas_call | solution.py:1079
  181.3 1.6 fusion
  182.9 1.8 convert_element_type.9
  184.7 1.0 slice_bitcast_fusion.2
  185.7 1.3 slice_reduce_fusion
  187.0 0.2 slice_bitcast_fusion
  187.2 1.2 copy.37
  188.3 0.0 copy-start.1
  188.3 0.0 copy-start
  188.3 1.2 copy.38
  189.5 0.7 slice.55
  190.2 0.6 reshape.56
  190.8 0.0 copy-done.1
  190.8 0.8 convert_element_type.8
  191.6 0.0 copy-done
  191.6 0.7 copy.40
  (1 shorter events, 0.0 us)
Async XLA Ops:
  188.3 2.5 %copy-start.1 = (bf16[192,512]{1,0:T(8,128)(2,1)S(1)}, bf16[192,512]{1,0:T(8,128)(2,1)}, u32[]{:S(2)}) copy-start(bf16[192,512]{1,0:T(8,128)(2,1)} %get-tuple-element.22) | copy-start | bytes 589828
  188.3 3.3 %copy-start = (bf16[192,512]{1,0:T(8,128)(2,1)S(1)}, bf16[192,512]{1,0:T(8,128)(2,1)}, u32[]{:S(2)}) copy-start(bf16[192,512]{1,0:T(8,128)(2,1)} %get-tuple-element.60) | copy-start | bytes 589828

commit v2 on v1

--- a/solution.py
+++ b/solution.py
@@ -278,6 +278,7 @@
 CHUNK = 384
 CHUNKS = 12
 SEMS = 256
+ORDER = (0, 3, 1, 2)
 
 
 def small_grid(mesh):
@@ -330,8 +331,7 @@
     G,
     R1,
     R2,
-    RD,
-    RU,
+    RZ,
     fin,
     xin,
     cin,
@@ -518,39 +518,56 @@
         return collect
 
     def gather(g):
-        zs, ys, cs = new("s", 6), new("s", 4), new("s", 8)
+        zs, ys, cs = new("s", 5), new("s", 4), new("s", 8)
         zr, yr, cr = new("r", 4), new("r", 4), new("r", 8)
         own, ychunk = 4 * g + dp, 4 * g + far
 
         def block(chunk, b):
             return W.at[chunk, rows(b)]
 
-        def up(d, b, pred):
-            start(pred, lambda: push(block(own, b), block(own, b), zs + d, zr + b, row=z + 1))
-
-        def down(d, b, pred):
-            start(pred, lambda: push(block(own, b), block(own, b), zs + 3 + d, zr + b, row=z - 1))
+        def along(n, b, to, pred):
+            start(pred, lambda: push(block(own, b), block(own, b), zs + n, zr + b, row=to))
 
         def first():
-            up(0, z, z < 3)
-            down(0, z, z > 0)
-
-        def hop(d):
-            for below in (True, False):
-                b = z - d if below else z + d
-                here = z >= d if below else z + d <= 3
-
-                @pl.when(here)
+            along(0, z, z + 1, (z < 3) if g == 0 else (z < 2))
+            along(1, z, z - 1, (z > 0) if g == 0 else (z > 1))
+            along(2, z, z + 2, z < 2)
+            along(3, z, z - 2, z > 1)
+
+        def late():
+            along(0, z, z + 1, z == 2)
+            along(1, z, z - 1, z == 1)
+
+        def take(b, pred):
+            @pl.when(pred)
+            def _():
+                arrived(block(own, b), zr + b, row=b)
+
+            start(pred, lambda: push(block(own, b), block(own, b), ys + b, yr + b, dp=far))
+            start(pred, lambda: push(block(own, b), block(own, b), cs + b, cr + b, dp=mate))
+
+        def hop1():
+            for b in range(4):
+                take(b, (z == b - 1) | (z == b + 1))
+
+        def hop2():
+            for b, at_ in ((0, 2), (3, 1)):
+
+                @pl.when(z == at_)
                 def _(b=b):
                     arrived(block(own, b), zr + b, row=b)
 
-                if d < 3:
-                    if below:
-                        up(d, b, here & (z < 3))
-                    else:
-                        down(d, b, here & (z > 0))
-                start(here, lambda b=b: push(block(own, b), block(own, b), ys + b, yr + b, dp=far))
-                start(here, lambda b=b: push(block(own, b), block(own, b), cs + b, cr + b, dp=mate))
+                along(4, b, 3 - b, z == at_)
+                start(z == at_, lambda b=b: push(block(own, b), block(own, b), ys + b, yr + b, dp=far))
+                start(z == at_, lambda b=b: push(block(own, b), block(own, b), cs + b, cr + b, dp=mate))
+            if g < 2:
+                gathers[g + 1][1]()
+            take(2, z == 0)
+            take(1, z == 3)
+
+        def hop3():
+            take(3, z == 0)
+            take(0, z == 3)
 
         def across():
             for b in range(4):
@@ -573,7 +590,7 @@
                     arrived(block(4 * g + mate, b), cr + b, dp=mate)
                     arrived(block(4 * g + matefar, b), cr + 4 + b, dp=mate)
 
-        return first, hop, across, finish
+        return first, late, hop1, hop2, hop3, across, finish
 
     def exchange(n):
         ssem, rsem = new("s", 3), new("r", 3)
@@ -593,10 +610,9 @@
         return jnp.concatenate(own, axis=1)
 
     def reduce(g):
-        s1_, s2_, sd, su, sy, sc = new("s", 2), new("s"), new("s", 3), new("s", 3), new("s"), new("s", 2)
-        r1, r2, rd, ru, ry, rc = new("r", 2), new("r"), new("r", 3), new("r", 3), new("r"), new("r", 2)
+        s1_, s2_, sz, sy, sc = new("s", 2), new("s", 4), new("s", 4), new("s"), new("s", 2)
+        r1, r2, rz, ry, rc = new("r", 2), new("r", 4), new("r", 4), new("r"), new("r", 2)
         own, ychunk = 4 * g + dp, 4 * g + far
-        sf = new("s", 2)
 
         def to_core():
             for j in range(2):
@@ -606,83 +622,41 @@
         def add(chunk, extra, base, count):
             def step(i):
                 at_ = pl.ds(pl.multiple_of(base + i * 64, 64), 64)
-                from_ = pl.ds(pl.multiple_of(i * 64, 64), 64)
-                G[chunk, at_, :] = (G[chunk, at_, :].astype(F32) + extra[from_, :].astype(F32)).astype(BF)
+                G[chunk, at_, :] = (G[chunk, at_, :].astype(F32) + extra[at_, :].astype(F32)).astype(BF)
 
             loop(count // 64, step)
 
+        def piece(ref, b):
+            return ref.at[pl.ds(b * ROWS, ROWS)]
+
         def to_y():
-            for j in (1 - y, y):
-                chunk = 4 * g + 2 * j + core
-                arrived(R1.at[g, j], r1 + j, dp=mate)
-                add(chunk, R1.at[g, j], 0, WIDE)
-                if j is not y:
-                    start(None, lambda: push(G.at[ychunk], R2.at[g], s2_, r2, dp=far))
-
-        def piece(b):
-            return G.at[own, rows(b)]
-
-        def send_down(b, pred):
-            start(pred, lambda: push(piece(b), RD.at[g, b], sd + b, rd + b, row=z - 1))
-
-        def send_up(b, pred):
-            start(pred, lambda: push(piece(b), RU.at[g, b - 1], su + b - 1, ru + b - 1, row=z + 1))
-
-        def take_down(b):
-            arrived(RD.at[g, b], rd + b, row=z + 1)
-            add(own, RD.at[g, b], b * ROWS, ROWS)
-
-        def take_up(b):
-            arrived(RU.at[g, b - 1], ru + b - 1, row=z - 1)
-            add(own, RU.at[g, b - 1], b * ROWS, ROWS)
-
-        def chain0():
-            arrived(R2.at[g], r2, dp=far)
-            add(own, R2.at[g], 0, WIDE)
-            for b in (0, 1, 2):
-                send_down(b, z == 3)
-            for b in (3, 2, 1):
-                send_up(b, z == 0)
-
-        def chain1():
-            for b in (0, 1):
-
-                @pl.when(z == 2)
-                def _(b=b):
-                    take_down(b)
-
-                send_down(b, z == 2)
-            for b in (3, 2):
-
-                @pl.when(z == 1)
-                def _(b=b):
-                    take_up(b)
-
-                send_up(b, z == 1)
-
-        def chain2():
-            @pl.when(z == 1)
-            def _():
-                take_down(0)
-
-            send_down(0, z == 1)
-
-            @pl.when(z == 2)
-            def _():
-                take_up(3)
-
-            send_up(3, z == 2)
+            arrived(R1.at[g, 1 - y], r1 + 1 - y, dp=mate)
+            for b in ORDER:
+                add(ychunk, R1.at[g, 1 - y], b * ROWS, ROWS)
+                start(
+                    None,
+                    lambda b=b: push(piece(G.at[ychunk], b), piece(R2.at[g], b), s2_ + b, r2 + b, dp=far),
+                )
+            arrived(R1.at[g, y], r1 + y, dp=mate)
+            add(own, R1.at[g, y], 0, WIDE)
+
+        def take(b):
+            arrived(piece(R2.at[g], b), r2 + b, dp=far)
+            add(own, R2.at[g], b * ROWS, ROWS)
+            start(z != b, lambda: push(piece(G.at[own], b), RZ.at[g, z], sz + b, rz + z, row=b))
 
         def settle():
-            @pl.when(z < 3)
-            def _():
-                take_down(z)
-
-            @pl.when(z > 0)
-            def _():
-                take_up(z)
-
-            fin[own] = G[own, mine, :]
+            for o in range(1, 4):
+                b = lax.rem(z + o, 4)
+                arrived(RZ.at[g, b], rz + b, row=b)
+            RZ[g, z] = G[own, mine, :]
+
+            def step(i):
+                at_ = pl.ds(pl.multiple_of(i * 32, 32), 32)
+                part = [RZ[g, b, at_, :].astype(F32) for b in range(4)]
+                fin[own, at_, :] = ((part[0] + part[1]) + (part[2] + part[3])).astype(BF)
+
+            loop(ROWS // 32, step)
             start(None, lambda: push(fin.at[own], fin.at[own], sy, ry, dp=far))
             start(None, lambda: push(fin.at[own], fin.at[own], sc, rc, dp=mate))
 
@@ -694,7 +668,7 @@
             arrived(fin.at[4 * g + mate], rc, dp=mate)
             arrived(fin.at[4 * g + matefar], rc + 1, dp=mate)
 
-        return to_core, to_y, chain0, chain1, chain2, settle, across, finish
+        return to_core, to_y, take, settle, across, finish
 
     def deliver(sent, landed, out):
         ssem, rsem = new("s", 4), new("r", 4)
@@ -746,20 +720,17 @@
     for g in range(3):
         gathers[g][0]()
     cot_in = spread(cot, cin)
+    gathers[0][2]()
     tok_in()
     tok_swap = swap(xin)
-    gathers[0][1](1)
-    gathers[0][1](2)
-    gathers[0][1](3)
+    gathers[0][3]()
+    gathers[0][4]()
+    vec_in()
     tok_swap()
-    vec_in()
     for h in range(2):
         xf[h * HALF : (h + 1) * HALF, :] = xin[h].astype(F32).T
-    gathers[0][2]()
-    gathers[1][1](1)
-    gathers[1][1](2)
-    gathers[1][1](3)
-    gathers[0][3]()
+    gathers[0][5]()
+    gathers[0][6]()
 
     xb = xf[...].astype(BF)
     for j, (dst, bias) in enumerate(((q, qb), (k, None), (v, vb))):
@@ -788,21 +759,21 @@
             outs.append(mm(pr.astype(BF), vv))
         at[p] = jnp.where(lane, outs[0], outs[1]).astype(BF)
 
+    gathers[1][2]()
     loop(3, attend)
-    gathers[2][1](1)
+    gathers[1][3]()
 
     put0, get0 = exchange(0)
     att = jnp.concatenate([at[0], at[1], at[2]], axis=1)
     for c in range(3):
         put0(c, mm_nt(att, W[3, c * SEQ : (c + 1) * SEQ, :]))
+    gathers[1][4]()
     for p in range(3):
         qT[p] = q[p].astype(F32).T.astype(BF)
         kT[p] = k[p].astype(F32).T.astype(BF)
-    gathers[2][1](2)
-    gathers[2][1](3)
-    gathers[1][2]()
-    cot_in()
-    cot_swap = swap(cin)
+    gathers[1][5]()
+    gathers[2][2]()
+    gathers[2][3]()
     get0()
 
     def norm1(i):
@@ -818,7 +789,7 @@
         hb[r, :] = h.astype(BF)
 
     loop(8, norm1)
-    gathers[1][3]()
+    gathers[1][6]()
 
     hv = hb[...]
     c0 = math.sqrt(2.0 / math.pi)
@@ -832,18 +803,21 @@
         dact[i] = half + (0.5 * u) * (1.0 - t * t) * (c0 * (1.0 + (3 * 0.044715) * u2))
 
     loop(4, up_step)
-    gathers[2][2]()
+    gathers[2][4]()
+    cot_in()
+    cot_swap = swap(cin)
+    gathers[2][5]()
     hT[...] = hid[...].T.astype(BF)
-    cot_swap()
-    for h in range(2):
-        cf[h * HALF : (h + 1) * HALF, :] = cin[h].astype(F32).T
-    gathers[2][3]()
+    gathers[2][6]()
     put1, get1 = exchange(1)
     for c in range(3):
         acc = mm_nt(act[0], W[8, c * SEQ : (c + 1) * SEQ, :])
         for i in range(1, 4):
             acc = acc + mm_nt(act[i], W[8 + i, c * SEQ : (c + 1) * SEQ, :])
         put1(c, acc)
+    cot_swap()
+    for h in range(2):
+        cf[h * HALF : (h + 1) * HALF, :] = cin[h].astype(F32).T
     get1()
 
     VA[...] = jnp.zeros_like(VA)
@@ -894,6 +868,7 @@
         prg[i] = low
 
     loop(4, pre_step)
+    reduces[2][1]()
     put2, get2 = exchange(2)
     for c in range(3):
         acc = mm_nt(prg[0], W[4, c * SEQ : (c + 1) * SEQ, :])
@@ -904,12 +879,12 @@
         VA[1 + i // 2 : 2 + i // 2, (i % 2) * CHUNK : (i % 2 + 1) * CHUNK] = mm(ones, prg[i])[0:1, :]
     loop(4, lambda i: outer(4 + i, hT, prg[i]))
     reduces[1][0]()
-    reduces[2][1]()
+    reduces[2][2](ORDER[0])
 
     mine_tokens = pl.ds(pl.multiple_of(x * HALF, HALF), HALF)
     osend[...] = outf[mine_tokens, :].T.astype(BF)
     out_in = deliver(osend, obuf, res_out)
-    reduces[2][2]()
+    reduces[2][2](ORDER[1])
     reduces[1][1]()
     get2()
 
@@ -935,8 +910,8 @@
         fgT[h] = t
         pgT[:, h * HALF : (h + 1) * HALF] = t.astype(BF)
 
-    reduces[2][3]()
-    reduces[1][2]()
+    reduces[2][2](ORDER[2])
+    reduces[2][2](ORDER[3])
     r = mm(pg[...], W[3])
     for p in range(3):
         part = r[:, p * HALF : (p + 1) * HALF].astype(BF)
@@ -961,8 +936,7 @@
         dT[2, p] = jnp.where(top, dv[0], dv[1]).astype(BF)
 
     loop(3, attend_back)
-    reduces[2][4]()
-    reduces[1][3]()
+    reduces[1][2](ORDER[0])
 
     for j in range(3):
         t = dT[j].reshape(CHUNK, SEQ)
@@ -991,29 +965,32 @@
     loop(3, back_step)
     ts, tr = new("s"), new("r")
     start(None, lambda: push(tgp.at[other], tgr, ts, tr, col=other))
-    reduces[0][1]()
-    reduces[2][5]()
-    reduces[1][4]()
     arrived(VB, vr, dp=mate)
     VD[...] = VA[...] + VB[...]
     start(None, lambda: push(VD, VC, vs + 1, vr + 1, dp=far))
-    reduces[0][2]()
+    reduces[2][3]()
+    reduces[0][1]()
+    reduces[1][2](ORDER[1])
     arrived(tgr, tr, col=other)
     tsend[...] = (tgp[x].astype(F32) + tgr[...].astype(F32) + fgT[x]).astype(BF)
     tg_in = deliver(tsend, tbuf, tg_out)
-    reduces[1][5]()
-    reduces[0][3]()
-    reduces[2][6]()
-    reduces[0][4]()
-    reduces[1][6]()
+    reduces[1][2](ORDER[2])
+    reduces[1][2](ORDER[3])
     arrived(VC, vr + 1, dp=far)
     VZ[z] = VD[...] + VC[...]
     for o in range(1, 4):
         to = lax.rem(z + o, 4)
         start(None, lambda o=o, to=to: push(VZ.at[z], VZ.at[z], vs + 1 + o, vr + 2 + z, row=to))
-    reduces[0][5]()
-    reduces[2][7]()
-    reduces[1][7]()
+    reduces[2][4]()
+    reduces[0][2](ORDER[0])
+    reduces[1][3]()
+    reduces[0][2](ORDER[1])
+    reduces[0][2](ORDER[2])
+    reduces[0][2](ORDER[3])
+    reduces[2][5]()
+    reduces[1][4]()
+    reduces[0][3]()
+    reduces[1][5]()
     copies = []
     fsem = new("s", 3)
 
@@ -1032,8 +1009,8 @@
     vec_out[...] = VZ[0] + VZ[1] + VZ[2] + VZ[3]
     copies += out_in()
     copies += tg_in()
-    reduces[0][6]()
-    reduces[0][7]()
+    reduces[0][4]()
+    reduces[0][5]()
     flush(0)
     for pred, make in pending:
         if pred is None:
@@ -1091,8 +1068,7 @@
             pltpu.VMEM((CHUNKS, WIDE, CHUNK), BF),
             pltpu.VMEM((3, 2, WIDE, CHUNK), BF),
             pltpu.VMEM((3, WIDE, CHUNK), BF),
-            pltpu.VMEM((3, 3, ROWS, CHUNK), BF),
-            pltpu.VMEM((3, 3, ROWS, CHUNK), BF),
+            pltpu.VMEM((3, 4, ROWS, CHUNK), BF),
             pltpu.VMEM((CHUNKS, ROWS, CHUNK), BF),
             pltpu.VMEM((2, WIDE, HALF), BF),
             pltpu.VMEM((2, WIDE, HALF), BF),

time: 195 us -> 174 us (0.89)
  Pallas kernels: 175 us -> 156 us
    pallas_call x1, Pallas kernels: 175 us -> 156 us  [fused_body(): pl.pallas_call(layer_kernel, out_shape=(jax.ShapeDtypeStruct((CHUNKS, ROW...]
where the time goes in v2:
time: 174 us; the launch traced here: 173 us
  Pallas kernels  156 us (90%)
  local copies, waits for them, and re-layouts  13 us (7%)
  other arithmetic  3.26 us (2%)
    pallas_call x1, Pallas kernels, fused_body(): pl.pallas_call(layer_kernel, out_shape=(jax.ShapeDtypeStruct((CHUNKS, ROW...  156 us

profile of v2, /device:TPU:17, one launch (start us, length us, event | category | flops | bytes accessed | tf_op | source)
XLA Modules:
  0.0 173.0 jit_solution(8858313967876183115)
XLA Ops:
  0.7 0.8 stack.27
  1.5 0.7 pad_maximum_fusion.own_vec
  2.2 1.3 reshape.54.ub
  3.5 1.2 reshape.52.qb
  4.7 1.2 reshape.53.vb
  5.9 156.1 %shard_map.305 = (bf16[12,192,384]{2,1,0:T(8,128)(2,1)}, bf16[192,512]{1,0:T(8,128)(2,1)}, bf16[192,512]{1,0:T(8,128)(2,1)}, f32[16,768]{1,0:T(8,128)}) custom-call(s32[1,256]{1,0:T(1,128)} %ids.1, bf16[192,512]{1,0:T(8,128)(2,1)} %tok.1, bf16[192,512]{1,0:T(8,128)(2,1)} %cot.1, bf16[192,384]{1,0:T(8,128)(2,1)} %qw.1, bf16[192,384]{1,0:T(8,128)(2,1)} %kw.1, ...), custom_call_target="tpu_custom_call" | custom-call | tf_op jit(solution)/shard_map/pallas_call | solution.py:1056
  162.0 1.6 fusion
  163.6 1.8 %convert_element_type.9 = f32[12,192,384]{2,1,0:T(8,128)S(1)} convert(bf16[12,192,384]{2,1,0:T(8,128)(2,1)} %get-tuple-element.23) | non-fusion elementwise | flops 884736 | bytes 5308416 | tf_op jit(solution)/shard_map/convert_element_type | solution.py:1140
  165.4 1.0 slice_bitcast_fusion.2
  166.4 1.3 slice_reduce_fusion
  167.7 0.2 slice_bitcast_fusion
  167.9 1.2 copy.37
  169.0 0.0 copy-start.1
  169.0 0.0 copy-start
  169.0 1.2 copy.38
  170.2 0.7 slice.55
  170.9 0.6 reshape.56
  171.5 0.0 copy-done.1
  171.5 0.8 convert_element_type.8
  172.3 0.0 copy-done
  172.3 0.7 copy.40
  (1 shorter events, 0.0 us)
Async XLA Ops:
  169.0 2.5 %copy-start.1 = (bf16[192,512]{1,0:T(8,128)(2,1)S(1)}, bf16[192,512]{1,0:T(8,128)(2,1)}, u32[]{:S(2)}) copy-start(bf16[192,512]{1,0:T(8,128)(2,1)} %get-tuple-element.22) | copy-start | bytes 589828
  169.0 3.3 %copy-start = (bf16[192,512]{1,0:T(8,128)(2,1)S(1)}, bf16[192,512]{1,0:T(8,128)(2,1)}, u32[]{:S(2)}) copy-start(bf16[192,512]{1,0:T(8,128)(2,1)} %get-tuple-element.60) | copy-start | bytes 589828

commit v3 on v2

--- a/solution.py
+++ b/solution.py
@@ -322,11 +322,24 @@
     qb,
     vb,
     ub,
-    own_vec,
-    fin_out,
+    ob,
+    ag,
+    ash,
+    db,
+    fgn,
+    fsh,
+    q_out,
+    k_out,
+    v_out,
+    o_out,
+    u_out,
+    d_out,
     res_out,
     tg_out,
-    vec_out,
+    bias_out,
+    norm_out,
+    own_vec,
+    upb,
     W,
     G,
     R1,
@@ -373,6 +386,8 @@
     dA,
     dAT,
     dT,
+    tcross,
+    ccross,
     tgp,
     tgr,
     osend,
@@ -454,45 +469,57 @@
     locals_ = local_parts()
     for c in locals_:
         c.start()
+    own_vec[...] = jnp.zeros_like(own_vec)
+    for n, ref in enumerate((ob, ag, ash, db, fgn, fsh)):
+        own_vec[n : n + 1, 0:ROWS] = ref[...].reshape(1, ROWS)
+    own_vec[...] = pltpu.roll(own_vec[...], z * ROWS, 1)
     vg[z] = own_vec[...]
+    for i in range(4):
+        upb[i] = ub[i * CHUNK : (i + 1) * CHUNK].reshape(1, CHUNK)
     seg = jnp.broadcast_to(ids[...].astype(F32), (SEQ, SEQ))
     neq[...] = jnp.abs(seg - seg.T)
     pl.semaphore_wait(bar, 9)
 
-    def spread(ref, landing):
-        ssem, rsem = new("s", 4), new("r", 4)
-        for s in range(2):
-            for h in range(2):
-                jj = 2 * x + s
-                self_ = (jj == z) & (h == x)
-                src = ref.at[:, s * SEQ + h * HALF : s * SEQ + (h + 1) * HALF]
-                dst = landing.at[h, mine]
-                start(
-                    jnp.logical_not(self_),
-                    lambda src=src, dst=dst, n=2 * s + h, jj=jj, h=h: push(
-                        src, dst, ssem + n, rsem + z, row=jj, col=h
-                    ),
-                )
-
-                @pl.when(self_)
-                def _(src=src, dst=dst):
-                    pltpu.make_async_copy(src, dst, recv.at[rsem + z]).start()
+    def spread(ref, landing, cross):
+        xs_, xr_, ssem, rsem = new("s", 2), new("r", 2), new("s", 8), new("r", 4)
+
+        def half(s, h):
+            return ref.at[:, pl.ds(pl.multiple_of(s * SEQ + h * HALF, HALF), HALF)]
+
+        def out(j, src, mine_):
+            n = ssem + j + (0 if mine_ else 4)
+            here = (x == j // 2) if mine_ else (x != j // 2)
+            start(here & (z != j), lambda: push(src, landing.at[x, mine], n, rsem + z, row=j))
+
+            @pl.when(here & (z == j))
+            def _():
+                pltpu.make_async_copy(src, landing.at[x, mine], recv.at[rsem + z]).start()
+
+        def begin():
+            for s in range(2):
+                start(None, lambda s=s: push(half(s, other), cross.at[s], xs_ + s, xr_ + s, col=other))
+            for j in range(4):
+                out(j, half(j % 2, x), True)
+
+        def relay():
+            for s in range(2):
+                arrived(cross.at[s], xr_ + s, col=other)
+            for j in range(4):
+                out(j, cross.at[j % 2], False)
 
         def collect():
-            home = lax.div(z, 2) == x
             for b in range(4):
-                local = home & (z == b)
                 dst = landing.at[x, rows(b)]
 
-                @pl.when(local)
+                @pl.when(z == b)
                 def _(dst=dst, b=b):
-                    pltpu.make_async_copy(ref.at[:, 0:HALF], dst, recv.at[rsem + b]).wait()
-
-                @pl.when(jnp.logical_not(local))
+                    pltpu.make_async_copy(cross.at[0], dst, recv.at[rsem + b]).wait()
+
+                @pl.when(z != b)
                 def _(dst=dst, b=b):
-                    arrived(dst, rsem + b, col=other)
-
-        return collect
+                    arrived(dst, rsem + b, row=b)
+
+        return begin, relay, collect
 
     def swap(landing):
         ssem, rsem = new("s"), new("r")
@@ -531,6 +558,8 @@
         def first():
             along(0, z, z + 1, (z < 3) if g == 0 else (z < 2))
             along(1, z, z - 1, (z > 0) if g == 0 else (z > 1))
+
+        def second():
             along(2, z, z + 2, z < 2)
             along(3, z, z - 2, z > 1)
 
@@ -590,7 +619,7 @@
                     arrived(block(4 * g + mate, b), cr + b, dp=mate)
                     arrived(block(4 * g + matefar, b), cr + 4 + b, dp=mate)
 
-        return first, late, hop1, hop2, hop3, across, finish
+        return (first, second), late, hop1, hop2, hop3, across, finish
 
     def exchange(n):
         ssem, rsem = new("s", 3), new("r", 3)
@@ -712,18 +741,23 @@
 
         return collect
 
-    tok_in = spread(tok, xin)
-    vec_in = share_vec()
+    tok_out, tok_relay, tok_in = spread(tok, xin, tcross)
+    tok_out()
     gathers = [gather(g) for g in range(3)]
     for c in locals_:
         c.wait()
-    for g in range(3):
-        gathers[g][0]()
-    cot_in = spread(cot, cin)
+    gathers[0][0][0]()
+    tok_relay()
+    gathers[0][0][1]()
+    vec_in = share_vec()
+    for g in range(1, 3):
+        gathers[g][0][0]()
+        gathers[g][0][1]()
+    cot_out, cot_relay, cot_in = spread(cot, cin, ccross)
     gathers[0][2]()
+    gathers[0][3]()
     tok_in()
     tok_swap = swap(xin)
-    gathers[0][3]()
     gathers[0][4]()
     vec_in()
     tok_swap()
@@ -736,7 +770,7 @@
     for j, (dst, bias) in enumerate(((q, qb), (k, None), (v, vb))):
         r = mm(xb, W[j])
         if bias is not None:
-            r = r + bias[...]
+            r = r + bias[...].reshape(1, CHUNK)
         for p in range(3):
             dst[p] = r[:, p * HALF : (p + 1) * HALF].astype(BF)
 
@@ -762,18 +796,19 @@
     gathers[1][2]()
     loop(3, attend)
     gathers[1][3]()
+    cot_out()
 
     put0, get0 = exchange(0)
     att = jnp.concatenate([at[0], at[1], at[2]], axis=1)
     for c in range(3):
         put0(c, mm_nt(att, W[3, c * SEQ : (c + 1) * SEQ, :]))
+    cot_relay()
     gathers[1][4]()
     for p in range(3):
         qT[p] = q[p].astype(F32).T.astype(BF)
         kT[p] = k[p].astype(F32).T.astype(BF)
     gathers[1][5]()
     gathers[2][2]()
-    gathers[2][3]()
     get0()
 
     def norm1(i):
@@ -789,13 +824,14 @@
         hb[r, :] = h.astype(BF)
 
     loop(8, norm1)
+    gathers[2][3]()
     gathers[1][6]()
 
     hv = hb[...]
     c0 = math.sqrt(2.0 / math.pi)
 
     def up_step(i):
-        u = mm(hv, W[4 + i]) + ub[i]
+        u = mm(hv, W[4 + i]) + upb[i]
         u2 = u * u
         t = jnp.tanh(c0 * (u + 0.044715 * (u2 * u)))
         half = 0.5 * (1.0 + t)
@@ -965,48 +1001,53 @@
     loop(3, back_step)
     ts, tr = new("s"), new("r")
     start(None, lambda: push(tgp.at[other], tgr, ts, tr, col=other))
+    reduces[1][2](ORDER[1])
     arrived(VB, vr, dp=mate)
     VD[...] = VA[...] + VB[...]
     start(None, lambda: push(VD, VC, vs + 1, vr + 1, dp=far))
-    reduces[2][3]()
     reduces[0][1]()
-    reduces[1][2](ORDER[1])
+    reduces[1][2](ORDER[2])
     arrived(tgr, tr, col=other)
     tsend[...] = (tgp[x].astype(F32) + tgr[...].astype(F32) + fgT[x]).astype(BF)
     tg_in = deliver(tsend, tbuf, tg_out)
-    reduces[1][2](ORDER[2])
     reduces[1][2](ORDER[3])
+    reduces[2][3]()
     arrived(VC, vr + 1, dp=far)
     VZ[z] = VD[...] + VC[...]
     for o in range(1, 4):
         to = lax.rem(z + o, 4)
         start(None, lambda o=o, to=to: push(VZ.at[z], VZ.at[z], vs + 1 + o, vr + 2 + z, row=to))
-    reduces[2][4]()
     reduces[0][2](ORDER[0])
+    reduces[0][2](ORDER[1])
     reduces[1][3]()
-    reduces[0][2](ORDER[1])
     reduces[0][2](ORDER[2])
     reduces[0][2](ORDER[3])
+    reduces[2][4]()
+    reduces[1][4]()
     reduces[2][5]()
-    reduces[1][4]()
+    reduces[1][5]()
     reduces[0][3]()
-    reduces[1][5]()
     copies = []
-    fsem = new("s", 3)
+    fsem = new("s", CHUNKS)
 
     def flush(g):
-        c = pltpu.make_async_copy(
-            fin.at[4 * g : 4 * g + 4], fin_out.at[4 * g : 4 * g + 4], send.at[fsem + g]
-        )
-        c.start()
-        copies.append(c)
+        for i in range(4):
+            if g == 0:
+                dst = (q_out, k_out, v_out, o_out)[i]
+            else:
+                dst = (u_out, d_out)[g - 1].at[:, i * CHUNK : (i + 1) * CHUNK]
+            c = pltpu.make_async_copy(fin.at[4 * g + i], dst, send.at[fsem + 4 * g + i])
+            c.start()
+            copies.append(c)
 
     flush(2)
     flush(1)
     for o in range(1, 4):
         b = lax.rem(z + o, 4)
         arrived(VZ.at[b], vr + 2 + b, row=b)
-    vec_out[...] = VZ[0] + VZ[1] + VZ[2] + VZ[3]
+    sums = VZ[0] + VZ[1] + VZ[2] + VZ[3]
+    bias_out[...] = sums[0:8, :]
+    norm_out[...] = pltpu.roll(sums, WIDE - z * ROWS, 1)[:, 0:SEQ]
     copies += out_in()
     copies += tg_in()
     reduces[0][4]()
@@ -1022,6 +1063,46 @@
                 make().wait_send()
 
     for c in copies:
+        c.wait()
+
+
+WIDTHS = (CHUNK,) * 4 + (4 * CHUNK,) * 2 + (2 * SEQ,)
+
+
+def widen_kernel(*refs):
+    count = len(WIDTHS)
+    ins, passed, bias, norm = refs[:count], refs[count], refs[count + 1], refs[count + 2]
+    refs = refs[count + 3 :]
+    outs, passed_out, vectors = refs[:count], refs[count], refs[count + 1 : count + 10]
+    refs = refs[count + 10 :]
+    low, wide, held, sem_in, sem_out = refs[:count], refs[count : 2 * count], *refs[2 * count :]
+    order = (4, 5, 6, 0, 1, 2, 3)
+    reads = {n: pltpu.make_async_copy(ins[n], low[n], sem_in.at[n]) for n in order}
+    through = pltpu.make_async_copy(passed, held, sem_in.at[count])
+    for n in order:
+        reads[n].start()
+    through.start()
+    vectors[0][...] = bias[0, 0:CHUNK]
+    vectors[1][...] = bias[0, CHUNK:WIDE]
+    for i in range(2):
+        vectors[2][i * WIDE : (i + 1) * WIDE] = bias[1 + i, :]
+    for n in range(6):
+        vectors[3 + n][...] = norm[3 + n, 0:ROWS]
+    writes = []
+    for n in order:
+        reads[n].wait()
+
+        def step(i, n=n):
+            r = pl.ds(pl.multiple_of(i * 32, 32), 32)
+            wide[n][r, :] = low[n][r, :].astype(F32)
+
+        loop(ROWS // 32, step)
+        writes.append(pltpu.make_async_copy(wide[n], outs[n], sem_out.at[n]))
+        writes[-1].start()
+    through.wait()
+    writes.append(pltpu.make_async_copy(held, passed_out, sem_out.at[count]))
+    writes[-1].start()
+    for c in writes:
         c.wait()
 
 
@@ -1045,25 +1126,22 @@
     ffn_shift,
     cotangent,
 ):
-    z = lax.axis_index("row")
-    vectors = jnp.stack([out_bias, attn_gain, attn_shift, down_bias, ffn_gain, ffn_shift])
-    vectors = jnp.pad(vectors, ((0, 2), (0, 0)))
-    placed = jnp.concatenate(
-        [jnp.where(z == b, vectors, 0.0) for b in range(4)], axis=1
-    )
     hbm = pl.BlockSpec(memory_space=pl.ANY)
     vmem = pl.BlockSpec(memory_space=pltpu.VMEM)
-    grads, out, tgrad, sums = pl.pallas_call(
+    gq, gk, gv, go, gu, gd, out, tgrad, bias, norm = pl.pallas_call(
         layer_kernel,
         out_shape=(
-            jax.ShapeDtypeStruct((CHUNKS, ROWS, CHUNK), BF),
-            jax.ShapeDtypeStruct((ROWS, 2 * SEQ), BF),
-            jax.ShapeDtypeStruct((ROWS, 2 * SEQ), BF),
-            jax.ShapeDtypeStruct((16, WIDE), F32),
+            *[jax.ShapeDtypeStruct((ROWS, CHUNK), BF)] * 4,
+            *[jax.ShapeDtypeStruct((ROWS, 4 * CHUNK), BF)] * 2,
+            *[jax.ShapeDtypeStruct((ROWS, 2 * SEQ), BF)] * 2,
+            jax.ShapeDtypeStruct((8, WIDE), F32),
+            jax.ShapeDtypeStruct((16, SEQ), F32),
         ),
-        in_specs=[vmem] + [hbm] * 8 + [vmem] * 4,
-        out_specs=(hbm, hbm, hbm, vmem),
+        in_specs=[vmem] + [hbm] * 8 + [vmem] * 9,
+        out_specs=(hbm,) * 8 + (vmem, vmem),
         scratch_shapes=[
+            pltpu.VMEM((8, WIDE), F32),
+            pltpu.VMEM((4, 1, CHUNK), F32),
             pltpu.VMEM((CHUNKS, WIDE, CHUNK), BF),
             pltpu.VMEM((CHUNKS, WIDE, CHUNK), BF),
             pltpu.VMEM((3, 2, WIDE, CHUNK), BF),
@@ -1110,6 +1188,8 @@
             pltpu.VMEM((3, SEQ, HALF), BF),
             pltpu.VMEM((3, HALF, SEQ), BF),
             pltpu.VMEM((3, 3, HALF, SEQ), BF),
+            pltpu.VMEM((2, ROWS, HALF), BF),
+            pltpu.VMEM((2, ROWS, HALF), BF),
             pltpu.VMEM((2, WIDE, HALF), BF),
             pltpu.VMEM((WIDE, HALF), BF),
             pltpu.VMEM((WIDE, HALF), BF),
@@ -1132,33 +1212,49 @@
         out_weight.T,
         up_weight,
         down_weight.T,
-        query_bias.reshape(1, CHUNK),
-        value_bias.reshape(1, CHUNK),
-        up_bias.reshape(4, 1, CHUNK),
-        placed,
-    )
-    wide = grads.astype(F32)
-    up_grad = wide[4:8].transpose(1, 0, 2).reshape(ROWS, 4 * CHUNK)
-    down_grad = wide[8:12].transpose(0, 2, 1).reshape(4 * CHUNK, ROWS)
-    slices = lax.dynamic_slice_in_dim(sums, z * ROWS, ROWS, 1)
+        query_bias,
+        value_bias,
+        up_bias,
+        out_bias,
+        attn_gain,
+        attn_shift,
+        down_bias,
+        ffn_gain,
+        ffn_shift,
+    )
+    count = len(WIDTHS)
+    sizes = (CHUNK, CHUNK, 4 * CHUNK) + (ROWS,) * 6
+    gq, gk, gv, go, gu, gd, tgrad, out, *vectors = pl.pallas_call(
+        widen_kernel,
+        out_shape=(
+            *[jax.ShapeDtypeStruct((ROWS, w), F32) for w in WIDTHS],
+            jax.ShapeDtypeStruct((ROWS, 2 * SEQ), BF),
+            *[jax.ShapeDtypeStruct((n,), F32) for n in sizes],
+        ),
+        in_specs=[hbm] * (count + 1) + [vmem] * 2,
+        out_specs=(hbm,) * (count + 1) + (vmem,) * len(sizes),
+        scratch_shapes=[
+            *[pltpu.VMEM((ROWS, w), BF) for w in WIDTHS],
+            *[pltpu.VMEM((ROWS, w), F32) for w in WIDTHS],
+            pltpu.VMEM((ROWS, 2 * SEQ), BF),
+            pltpu.SemaphoreType.DMA((count + 1,)),
+            pltpu.SemaphoreType.DMA((count + 1,)),
+        ],
+    )(gq, gk, gv, go, gu, gd, tgrad, out, bias, norm)
     return (
         out,
-        tgrad.astype(F32),
-        wide[0],
-        wide[1],
-        wide[2],
-        sums[0, :CHUNK],
-        sums[0, CHUNK:],
-        wide[3].T,
-        slices[3],
-        slices[4],
-        slices[5],
-        up_grad,
-        sums[1:3].reshape(4 * CHUNK),
-        down_grad,
-        slices[6],
-        slices[7],
-        slices[8],
+        tgrad,
+        gq,
+        gk,
+        gv,
+        vectors[0],
+        vectors[1],
+        go.T,
+        *vectors[3:6],
+        gu,
+        vectors[2],
+        gd.T,
+        *vectors[6:9],
     )
 
 

time: 174 us -> 151 us (0.87)
  local copies, waits for them, and re-layouts: 13 us -> 0 us
  Pallas kernels: 156 us -> 150 us
  other arithmetic: 3.26 us -> 0 us
    reshape x6 -> x0, local copies, waits for them, and re-layouts: 6.71 us -> none  [the longest x1 1.3 us: fused_body(): up_bias.reshape(4, 1, CHUNK)]
    pallas_call x1 -> x2, Pallas kernels: 156 us -> 150 us  [the longest x1 145 us: fused_body(): pl.pallas_call(layer_kernel, out_shape=(*[jax.ShapeDtypeStruct((ROWS, CHU...]
    slice x3 -> x0, local copies, waits for them, and re-layouts: 3.63 us -> none  [the longest x1 1.57 us: fused_body(): slices[8]]
    convert_element_type x2 -> x0, other arithmetic: 2.57 us -> none  [the longest x1 1.78 us: fused_body(): wide = grads.astype(F32)]
where the time goes in v3:
time: 151 us; the launch traced here: 150 us
  Pallas kernels  150 us (99%)
    pallas_call x1, Pallas kernels, fused_body(): pl.pallas_call(layer_kernel, out_shape=(*[jax.ShapeDtypeStruct((ROWS, CHU...  145 us
    pallas_call x1, Pallas kernels, fused_body(): pl.pallas_call(widen_kernel, out_shape=(*[jax.ShapeDtypeStruct((ROWS, w),...  4.65 us

profile of v3, /device:TPU:17, one launch (start us, length us, event | category | flops | bytes accessed | tf_op | source)
XLA Modules:
  0.0 150.5 jit_solution(11959994303660067999)
XLA Ops:
  0.7 145.2 %shard_map.305 = (bf16[192,384]{1,0:T(8,128)(2,1)}, bf16[192,384]{1,0:T(8,128)(2,1)}, bf16[192,384]{1,0:T(8,128)(2,1)}, bf16[192,384]{1,0:T(8,128)(2,1)}, bf16[1...) custom-call(s32[1,256]{1,0:T(1,128)} %ids.1, ...), custom_call_target="tpu_custom_call" | custom-call | tf_op jit(solution)/shard_map/pallas_call | solution.py:1131
  145.8 4.7 %shard_map.306 = (f32[192,384]{1,0:T(8,128)}, f32[192,384]{1,0:T(8,128)}, f32[192,384]{1,0:T(8,128)}, f32[192,384]{1,0:T(8,128)}, f32[192,1536]{1,0:T(8,128)}, /...) custom-call(bf16[192,384]{1,0:T(8,128)(2,1)} %get-tuple-element.44.r, ...), custom_call_target="tpu_custom_call" | custom-call | tf_op jit(solution)/shard_map/pallas_call | solution.py:1227

commit v4 on v3

--- a/solution.py
+++ b/solution.py
@@ -274,6 +274,7 @@
 SEQ = 256
 WIDE = 768
 HALF = 128
+PART = 64
 ROWS = 192
 CHUNK = 384
 CHUNKS = 12
@@ -350,6 +351,7 @@
     cin,
     xs,
     xr,
+    RX,
     vg,
     vec,
     VA,
@@ -575,9 +577,13 @@
             start(pred, lambda: push(block(own, b), block(own, b), ys + b, yr + b, dp=far))
             start(pred, lambda: push(block(own, b), block(own, b), cs + b, cr + b, dp=mate))
 
-        def hop1():
-            for b in range(4):
-                take(b, (z == b - 1) | (z == b + 1))
+        def hop1(ends=None):
+            if ends is not False:
+                take(1, z == 0)
+                take(2, z == 3)
+            if ends is not True:
+                for b in range(4):
+                    take(b, ((z == b - 1) | (z == b + 1)) & ((z == 1) | (z == 2)))
 
         def hop2():
             for b, at_ in ((0, 2), (3, 1)):
@@ -591,6 +597,8 @@
                 start(z == at_, lambda b=b: push(block(own, b), block(own, b), cs + b, cr + b, dp=mate))
             if g < 2:
                 gathers[g + 1][1]()
+
+        def hop2_ends():
             take(2, z == 0)
             take(1, z == 3)
 
@@ -619,34 +627,46 @@
                     arrived(block(4 * g + mate, b), cr + b, dp=mate)
                     arrived(block(4 * g + matefar, b), cr + 4 + b, dp=mate)
 
-        return (first, second), late, hop1, hop2, hop3, across, finish
+        return (first, second), late, hop1, hop2, hop3, across, finish, hop2_ends
 
     def exchange(n):
-        ssem, rsem = new("s", 3), new("r", 3)
-
-        def put(c, value):
-            xs[n, c] = value.astype(BF)
-            start(None, lambda: push(xs.at[n, c], xr.at[n, c], ssem + c, rsem + c, col=other))
-
-        def collect():
-            for c in range(3):
-                arrived(xr.at[n, c], rsem + c, col=other)
-
-        return put, collect
+        ssem, rsem = new("s", 4), new("r", 4)
+
+        def quarter(ref, i):
+            return ref.at[n, pl.ds(pl.multiple_of(i * PART, PART), PART)]
+
+        def put(h, value):
+            xs[n, h * HALF : (h + 1) * HALF, :] = value.astype(BF)
+            for i in (2 * h, 2 * h + 1):
+                start(
+                    None,
+                    lambda i=i: push(quarter(xs, i), quarter(xr, i), ssem + i, rsem + i, col=other),
+                )
+
+        def get(i):
+            arrived(quarter(xr, i), rsem + i, col=other)
+
+        return put, get
 
     def both(n, r):
-        own = [xs[n, c, r, :].astype(F32) + xr[n, c, r, :].astype(F32) for c in range(3)]
-        return jnp.concatenate(own, axis=1)
+        return xs[n, r, :].astype(F32) + xr[n, r, :].astype(F32)
+
+    def by_quarter(get, step, carry):
+        def quarter(i, carry):
+            get(i)
+            return lax.fori_loop(0, 2, lambda j, c: step(2 * i + j, c), carry)
+
+        return lax.fori_loop(0, 4, quarter, carry)
 
     def reduce(g):
+        rx = new("r")
         s1_, s2_, sz, sy, sc = new("s", 2), new("s", 4), new("s", 4), new("s"), new("s", 2)
         r1, r2, rz, ry, rc = new("r", 2), new("r", 4), new("r", 4), new("r"), new("r", 2)
         own, ychunk = 4 * g + dp, 4 * g + far
 
-        def to_core():
-            for j in range(2):
-                src = G.at[4 * g + 2 * j + 1 - core]
-                start(None, lambda src=src, j=j: push(src, R1.at[g, j], s1_ + j, r1 + j, dp=mate))
+        def to_core(j):
+            src = G.at[4 * g + 2 * j + 1 - core]
+            start(None, lambda: push(src, R1.at[g, j], s1_ + j, r1 + j, dp=mate))
 
         def add(chunk, extra, base, count):
             def step(i):
@@ -669,15 +689,51 @@
             arrived(R1.at[g, y], r1 + y, dp=mate)
             add(own, R1.at[g, y], 0, WIDE)
 
+        def send(b, pred):
+            start(pred, lambda: push(piece(G.at[own], b), RZ.at[g, z], sz + b, rz + z, row=b))
+
         def take(b):
             arrived(piece(R2.at[g], b), r2 + b, dp=far)
             add(own, R2.at[g], b * ROWS, ROWS)
-            start(z != b, lambda: push(piece(G.at[own], b), RZ.at[g, z], sz + b, rz + z, row=b))
+            if b in (1, 2):
+                send(b, z != b)
+            else:
+                send(b, z == (1 if b == 0 else 2))
+                start(
+                    z == 3 - b,
+                    lambda: push(piece(G.at[own], b), RX.at[g], sz + b, rx, row=2 if b == 0 else 1),
+                )
+
+        def relay(b):
+            here = z == (2 if b == 0 else 1)
+
+            @pl.when(here)
+            def _():
+                arrived(RX.at[g], rx, row=3 - b)
+
+                def step(i):
+                    at_ = pl.ds(pl.multiple_of(b * ROWS + i * 64, 64), 64)
+                    from_ = pl.ds(pl.multiple_of(i * 64, 64), 64)
+                    G[own, at_, :] = (G[own, at_, :].astype(F32) + RX[g, from_, :].astype(F32)).astype(BF)
+
+                loop(ROWS // 64, step)
+
+            send(b, here)
 
         def settle():
-            for o in range(1, 4):
-                b = lax.rem(z + o, 4)
-                arrived(RZ.at[g, b], rz + b, row=b)
+            for b in range(4):
+                if b in (0, 3):
+
+                    @pl.when(z == 3 - b)
+                    def _(b=b):
+                        RZ[g, b] = jnp.zeros((ROWS, CHUNK), BF)
+
+                there = (z != b) & (z != 3 - b) if b in (0, 3) else z != b
+
+                @pl.when(there)
+                def _(b=b):
+                    arrived(RZ.at[g, b], rz + b, row=b)
+
             RZ[g, z] = G[own, mine, :]
 
             def step(i):
@@ -697,7 +753,7 @@
             arrived(fin.at[4 * g + mate], rc, dp=mate)
             arrived(fin.at[4 * g + matefar], rc + 1, dp=mate)
 
-        return to_core, to_y, take, settle, across, finish
+        return to_core, to_y, take, settle, across, finish, relay
 
     def deliver(sent, landed, out):
         ssem, rsem = new("s", 4), new("r", 4)
@@ -756,9 +812,12 @@
     cot_out, cot_relay, cot_in = spread(cot, cin, ccross)
     gathers[0][2]()
     gathers[0][3]()
+    gathers[0][7]()
     tok_in()
     tok_swap = swap(xin)
     gathers[0][4]()
+    gathers[1][3]()
+    gathers[1][2](True)
     vec_in()
     tok_swap()
     for h in range(2):
@@ -793,25 +852,25 @@
             outs.append(mm(pr.astype(BF), vv))
         at[p] = jnp.where(lane, outs[0], outs[1]).astype(BF)
 
-    gathers[1][2]()
+    gathers[1][2](False)
+    gathers[1][7]()
     loop(3, attend)
-    gathers[1][3]()
+    gathers[2][3]()
     cot_out()
+    gathers[1][4]()
 
     put0, get0 = exchange(0)
     att = jnp.concatenate([at[0], at[1], at[2]], axis=1)
-    for c in range(3):
-        put0(c, mm_nt(att, W[3, c * SEQ : (c + 1) * SEQ, :]))
+    for h in range(2):
+        put0(h, mm_nt(att[h * HALF : (h + 1) * HALF, :], W[3]))
+    gathers[2][2](True)
     cot_relay()
-    gathers[1][4]()
     for p in range(3):
         qT[p] = q[p].astype(F32).T.astype(BF)
         kT[p] = k[p].astype(F32).T.astype(BF)
     gathers[1][5]()
-    gathers[2][2]()
-    get0()
-
-    def norm1(i):
+    gathers[2][2](False)
+    def norm1(i, carry):
         r = pl.ds(pl.multiple_of(i * 32, 32), 32)
         resid = xf[r, :] + (both(0, r) + vec[0:1, :])
         d = resid - row_mean(resid)
@@ -822,9 +881,11 @@
         s1[r, :] = jnp.broadcast_to(s, (32, HALF))
         hid[r, :] = h
         hb[r, :] = h.astype(BF)
-
-    loop(8, norm1)
-    gathers[2][3]()
+        return carry
+
+    gathers[2][7]()
+    gathers[2][4]()
+    by_quarter(get0, norm1, 0)
     gathers[1][6]()
 
     hv = hb[...]
@@ -839,22 +900,21 @@
         dact[i] = half + (0.5 * u) * (1.0 - t * t) * (c0 * (1.0 + (3 * 0.044715) * u2))
 
     loop(4, up_step)
-    gathers[2][4]()
     cot_in()
     cot_swap = swap(cin)
     gathers[2][5]()
     hT[...] = hid[...].T.astype(BF)
     gathers[2][6]()
     put1, get1 = exchange(1)
-    for c in range(3):
-        acc = mm_nt(act[0], W[8, c * SEQ : (c + 1) * SEQ, :])
+    for h in range(2):
+        half = slice(h * HALF, (h + 1) * HALF)
+        acc = mm_nt(act[0, half, :], W[8])
         for i in range(1, 4):
-            acc = acc + mm_nt(act[i], W[8 + i, c * SEQ : (c + 1) * SEQ, :])
-        put1(c, acc)
+            acc = acc + mm_nt(act[i, half, :], W[8 + i])
+        put1(h, acc)
     cot_swap()
     for h in range(2):
         cf[h * HALF : (h + 1) * HALF, :] = cin[h].astype(F32).T
-    get1()
 
     VA[...] = jnp.zeros_like(VA)
 
@@ -875,7 +935,7 @@
         return gain_sum + fold(up * n), shift_sum + fold(up), bias_sum + fold(low.astype(F32))
 
     zero = jnp.zeros((8, WIDE), F32)
-    sums = lax.fori_loop(0, 8, norm2, (zero, zero, zero))
+    sums = by_quarter(get1, norm2, (zero, zero, zero))
 
     def total(values):
         return jnp.sum(values, axis=0, keepdims=True)
@@ -893,8 +953,16 @@
 
         loop(3, step)
 
-    loop(4, lambda i: outer(8 + i, dgT, act[i]))
-    reduces[2][0]()
+    def products(g, left, rights):
+        for to in (1 - core, core):
+            for j in (1 - y, y):
+                i = 2 * j + to
+                outer(4 * g + i, left, rights[i])
+                if to is not core:
+                    reduces[g][0](j)
+
+    products(2, dgT, act)
+    reduces[2][1]()
 
     ones = jnp.ones((8, SEQ), BF)
     dgv = dg[...]
@@ -904,17 +972,16 @@
         prg[i] = low
 
     loop(4, pre_step)
-    reduces[2][1]()
     put2, get2 = exchange(2)
-    for c in range(3):
-        acc = mm_nt(prg[0], W[4, c * SEQ : (c + 1) * SEQ, :])
+    for h in range(2):
+        half = slice(h * HALF, (h + 1) * HALF)
+        acc = mm_nt(prg[0, half, :], W[4])
         for i in range(1, 4):
-            acc = acc + mm_nt(prg[i], W[4 + i, c * SEQ : (c + 1) * SEQ, :])
-        put2(c, acc)
+            acc = acc + mm_nt(prg[i, half, :], W[4 + i])
+        put2(h, acc)
     for i in range(4):
         VA[1 + i // 2 : 2 + i // 2, (i % 2) * CHUNK : (i % 2 + 1) * CHUNK] = mm(ones, prg[i])[0:1, :]
-    loop(4, lambda i: outer(4 + i, hT, prg[i]))
-    reduces[1][0]()
+    products(1, hT, prg)
     reduces[2][2](ORDER[0])
 
     mine_tokens = pl.ds(pl.multiple_of(x * HALF, HALF), HALF)
@@ -922,7 +989,6 @@
     out_in = deliver(osend, obuf, res_out)
     reduces[2][2](ORDER[1])
     reduces[1][1]()
-    get2()
 
     def norm1_back(i, carry):
         gain_sum, shift_sum, bias_sum = carry
@@ -937,7 +1003,7 @@
         pg[r, :] = low
         return gain_sum + fold(up * n), shift_sum + fold(up), bias_sum + fold(low.astype(F32))
 
-    sums = lax.fori_loop(0, 8, norm1_back, (zero, zero, zero))
+    sums = by_quarter(get2, norm1_back, (zero, zero, zero))
     VA[4:5, :] = total(sums[0])
     VA[5:6, :] = total(sums[1])
     VA[3:4, :] = total(sums[2])
@@ -947,6 +1013,7 @@
         pgT[:, h * HALF : (h + 1) * HALF] = t.astype(BF)
 
     reduces[2][2](ORDER[2])
+    reduces[2][6](ORDER[0])
     reduces[2][2](ORDER[3])
     r = mm(pg[...], W[3])
     for p in range(3):
@@ -972,6 +1039,7 @@
         dT[2, p] = jnp.where(top, dv[0], dv[1]).astype(BF)
 
     loop(3, attend_back)
+    reduces[2][6](ORDER[1])
     reduces[1][2](ORDER[0])
 
     for j in range(3):
@@ -986,9 +1054,10 @@
             G[j, r, :] = mm_nt(left, t).astype(BF)
 
         loop(3, step)
-    reduces[0][0]()
     vs, vr = new("s", 5), new("r", 6)
     start(None, lambda: push(VA, VB, vs, vr, dp=mate))
+    reduces[0][0](1 - y)
+    reduces[0][0](y)
 
     def back_step(b):
         r = pl.ds(pl.multiple_of(b * SEQ, SEQ), SEQ)
@@ -1007,10 +1076,12 @@
     start(None, lambda: push(VD, VC, vs + 1, vr + 1, dp=far))
     reduces[0][1]()
     reduces[1][2](ORDER[2])
+    reduces[1][6](ORDER[0])
+    reduces[1][2](ORDER[3])
+    reduces[1][6](ORDER[1])
     arrived(tgr, tr, col=other)
     tsend[...] = (tgp[x].astype(F32) + tgr[...].astype(F32) + fgT[x]).astype(BF)
     tg_in = deliver(tsend, tbuf, tg_out)
-    reduces[1][2](ORDER[3])
     reduces[2][3]()
     arrived(VC, vr + 1, dp=far)
     VZ[z] = VD[...] + VC[...]
@@ -1019,14 +1090,16 @@
         start(None, lambda o=o, to=to: push(VZ.at[z], VZ.at[z], vs + 1 + o, vr + 2 + z, row=to))
     reduces[0][2](ORDER[0])
     reduces[0][2](ORDER[1])
+    reduces[0][2](ORDER[2])
+    reduces[0][6](ORDER[0])
+    reduces[0][2](ORDER[3])
+    reduces[0][6](ORDER[1])
     reduces[1][3]()
-    reduces[0][2](ORDER[2])
-    reduces[0][2](ORDER[3])
     reduces[2][4]()
     reduces[1][4]()
     reduces[2][5]()
+    reduces[0][3]()
     reduces[1][5]()
-    reduces[0][3]()
     copies = []
     fsem = new("s", CHUNKS)
 
@@ -1150,8 +1223,9 @@
             pltpu.VMEM((CHUNKS, ROWS, CHUNK), BF),
             pltpu.VMEM((2, WIDE, HALF), BF),
             pltpu.VMEM((2, WIDE, HALF), BF),
-            pltpu.VMEM((3, 3, SEQ, SEQ), BF),
-            pltpu.VMEM((3, 3, SEQ, SEQ), BF),
+            pltpu.VMEM((3, SEQ, WIDE), BF),
+            pltpu.VMEM((3, SEQ, WIDE), BF),
+            pltpu.VMEM((3, ROWS, CHUNK), BF),
             pltpu.VMEM((4, 8, WIDE), F32),
             pltpu.VMEM((8, WIDE), F32),
             pltpu.VMEM((16, WIDE), F32),

time: 151 us -> 141 us (0.934)
  the two profiles are of different devices: /device:TPU:17 before, /device:TPU:1 now
where the time goes in v4:
time: 141 us
  Pallas kernels  140 us (99%)
    pallas_call x1, Pallas kernels, fused_body(): pl.pallas_call(layer_kernel, out_shape=(*[jax.ShapeDtypeStruct((ROWS, CHU...  136 us
    pallas_call x1, Pallas kernels, fused_body(): pl.pallas_call(widen_kernel, out_shape=(*[jax.ShapeDtypeStruct((ROWS, w),...  4.65 us

profile of v4, /device:TPU:1, one launch (start us, length us, event | category | flops | bytes accessed | tf_op | source)
XLA Modules:
  0.0 141.1 jit_solution(223749828703086706)
XLA Ops:
  0.7 135.8 %shard_map.305 = (bf16[192,384]{1,0:T(8,128)(2,1)}, bf16[192,384]{1,0:T(8,128)(2,1)}, bf16[192,384]{1,0:T(8,128)(2,1)}, bf16[192,384]{1,0:T(8,128)(2,1)}, bf16[1...) custom-call(s32[1,256]{1,0:T(1,128)} %ids.1, ...), custom_call_target="tpu_custom_call" | custom-call | tf_op jit(solution)/shard_map/pallas_call | solution.py:1204
  136.4 4.7 %shard_map.306 = (f32[192,384]{1,0:T(8,128)}, f32[192,384]{1,0:T(8,128)}, f32[192,384]{1,0:T(8,128)}, f32[192,384]{1,0:T(8,128)}, f32[192,1536]{1,0:T(8,128)}, /...) custom-call(bf16[192,384]{1,0:T(8,128)(2,1)} %get-tuple-element.44.r, ...), custom_call_target="tpu_custom_call" | custom-call | tf_op jit(solution)/shard_map/pallas_call | solution.py:1301

commit v5 on v4

--- a/solution.py
+++ b/solution.py
@@ -500,6 +500,8 @@
         def begin():
             for s in range(2):
                 start(None, lambda s=s: push(half(s, other), cross.at[s], xs_ + s, xr_ + s, col=other))
+
+        def along():
             for j in range(4):
                 out(j, half(j % 2, x), True)
 
@@ -521,7 +523,7 @@
                 def _(dst=dst, b=b):
                     arrived(dst, rsem + b, row=b)
 
-        return begin, relay, collect
+        return begin, along, relay, collect
 
     def swap(landing):
         ssem, rsem = new("s"), new("r")
@@ -797,8 +799,9 @@
 
         return collect
 
-    tok_out, tok_relay, tok_in = spread(tok, xin, tcross)
+    tok_out, tok_along, tok_relay, tok_in = spread(tok, xin, tcross)
     tok_out()
+    tok_along()
     gathers = [gather(g) for g in range(3)]
     for c in locals_:
         c.wait()
@@ -809,20 +812,20 @@
     for g in range(1, 3):
         gathers[g][0][0]()
         gathers[g][0][1]()
-    cot_out, cot_relay, cot_in = spread(cot, cin, ccross)
+    cot_out, cot_along, cot_relay, cot_in = spread(cot, cin, ccross)
     gathers[0][2]()
     gathers[0][3]()
-    gathers[0][7]()
     tok_in()
     tok_swap = swap(xin)
+    cot_out()
+    gathers[0][7]()
     gathers[0][4]()
     gathers[1][3]()
-    gathers[1][2](True)
-    vec_in()
     tok_swap()
     for h in range(2):
         xf[h * HALF : (h + 1) * HALF, :] = xin[h].astype(F32).T
     gathers[0][5]()
+    gathers[1][2](True)
     gathers[0][6]()
 
     xb = xf[...].astype(BF)
@@ -856,7 +859,6 @@
     gathers[1][7]()
     loop(3, attend)
     gathers[2][3]()
-    cot_out()
     gathers[1][4]()
 
     put0, get0 = exchange(0)
@@ -864,6 +866,7 @@
     for h in range(2):
         put0(h, mm_nt(att[h * HALF : (h + 1) * HALF, :], W[3]))
     gathers[2][2](True)
+    cot_along()
     cot_relay()
     for p in range(3):
         qT[p] = q[p].astype(F32).T.astype(BF)
@@ -885,7 +888,10 @@
 
     gathers[2][7]()
     gathers[2][4]()
+    vec_in()
     by_quarter(get0, norm1, 0)
+    cot_in()
+    cot_swap = swap(cin)
     gathers[1][6]()
 
     hv = hb[...]
@@ -900,8 +906,6 @@
         dact[i] = half + (0.5 * u) * (1.0 - t * t) * (c0 * (1.0 + (3 * 0.044715) * u2))
 
     loop(4, up_step)
-    cot_in()
-    cot_swap = swap(cin)
     gathers[2][5]()
     hT[...] = hid[...].T.astype(BF)
     gathers[2][6]()
@@ -1079,21 +1083,21 @@
     reduces[1][6](ORDER[0])
     reduces[1][2](ORDER[3])
     reduces[1][6](ORDER[1])
-    arrived(tgr, tr, col=other)
-    tsend[...] = (tgp[x].astype(F32) + tgr[...].astype(F32) + fgT[x]).astype(BF)
-    tg_in = deliver(tsend, tbuf, tg_out)
     reduces[2][3]()
-    arrived(VC, vr + 1, dp=far)
-    VZ[z] = VD[...] + VC[...]
-    for o in range(1, 4):
-        to = lax.rem(z + o, 4)
-        start(None, lambda o=o, to=to: push(VZ.at[z], VZ.at[z], vs + 1 + o, vr + 2 + z, row=to))
     reduces[0][2](ORDER[0])
     reduces[0][2](ORDER[1])
     reduces[0][2](ORDER[2])
     reduces[0][6](ORDER[0])
     reduces[0][2](ORDER[3])
     reduces[0][6](ORDER[1])
+    arrived(tgr, tr, col=other)
+    tsend[...] = (tgp[x].astype(F32) + tgr[...].astype(F32) + fgT[x]).astype(BF)
+    tg_in = deliver(tsend, tbuf, tg_out)
+    arrived(VC, vr + 1, dp=far)
+    VZ[z] = VD[...] + VC[...]
+    for o in range(1, 4):
+        to = lax.rem(z + o, 4)
+        start(None, lambda o=o, to=to: push(VZ.at[z], VZ.at[z], vs + 1 + o, vr + 2 + z, row=to))
     reduces[1][3]()
     reduces[2][4]()
     reduces[1][4]()

time: 141 us -> 138 us (0.979)
  the two profiles are of different devices: /device:TPU:1 before, /device:TPU:17 now
where the time goes in v5:
time: 138 us; the launch traced here: 136 us
  Pallas kernels  135 us (98%)
    pallas_call x1, Pallas kernels, fused_body(): pl.pallas_call(layer_kernel, out_shape=(*[jax.ShapeDtypeStruct((ROWS, CHU...  131 us
    pallas_call x1, Pallas kernels, fused_body(): pl.pallas_call(widen_kernel, out_shape=(*[jax.ShapeDtypeStruct((ROWS, w),...  4.65 us

profile of v5, /device:TPU:17, one launch (start us, length us, event | category | flops | bytes accessed | tf_op | source)
XLA Modules:
  0.0 136.0 jit_solution(18190358022390063231)
XLA Ops:
  0.7 130.7 %shard_map.305 = (bf16[192,384]{1,0:T(8,128)(2,1)}, bf16[192,384]{1,0:T(8,128)(2,1)}, bf16[192,384]{1,0:T(8,128)(2,1)}, bf16[192,384]{1,0:T(8,128)(2,1)}, bf16[1...) custom-call(s32[1,256]{1,0:T(1,128)} %ids.1, ...), custom_call_target="tpu_custom_call" | custom-call | tf_op jit(solution)/shard_map/pallas_call | solution.py:1208
  131.4 4.7 %shard_map.306 = (f32[192,384]{1,0:T(8,128)}, f32[192,384]{1,0:T(8,128)}, f32[192,384]{1,0:T(8,128)}, f32[192,384]{1,0:T(8,128)}, f32[192,1536]{1,0:T(8,128)}, /...) custom-call(bf16[192,384]{1,0:T(8,128)(2,1)} %get-tuple-element.44.r, ...), custom_call_target="tpu_custom_call" | custom-call | tf_op jit(solution)/shard_map/pallas_call | solution.py:1305
